TPU v7x, 32 devices: a whole 2x2x4 slice. The times are simulated.
32 devices in a mesh: layer: 4 (over y, core), front: 8 (over z, x).
Axes of the slice: x: 2, y: 2, z: 4, core: 2. Of those that a mesh axis runs over, the one named last changes fastest.
Arguments:
- child_rhs: bfloat16 [4, 2, 48, 8192], P('layer', None, None, 'front'), may hold values from -6 to 6
- parent_rhs: bfloat16 [4, 2, 48, 4096], P('layer', None, None, 'front'), may hold values from -6 to 6
- root_rhs: bfloat16 [4, 2, 48, 4096], P('layer', None, None, 'front'), may hold values from -6 to 6
- child_inverse: bfloat16 [4, 2048, 8192], P('layer', None, 'front'), as said below
- child_update: bfloat16 [4, 8192, 2048], P('layer', 'front'), may hold values from -0.125 to 0.125
- parent_inverse: bfloat16 [4, 2048, 4096], P('layer', None, 'front'), as said below
- parent_update: bfloat16 [4, 4096, 3072], P('layer', 'front'), may hold values from -0.125 to 0.125
- root_inverse: bfloat16 [4, 4096, 4096], P('layer', None, 'front'), as said below
- coupling: float32 [4, 4096], P('layer', 'front'), may hold values from 0.25 to 1
- child_map: int32 [4, 2048], replicated, may hold values from 0 to 6143, as said below
- parent_map: int32 [2, 3072], replicated, may hold values from 0 to 4095, as said below
Outputs:
- solution: bfloat16 [4, 2, 48, 4096], P('layer', None, None, 'front')
Inputs may be any that keep to these rules, and one draw needn't show every extreme that they name: `child_map`: each row holds 2048 distinct entries; values below 2048 name rows of the parent front's separator, the others name row value - 2048 of the top separator. `parent_map`: each row holds 3072 distinct rows of the top separator. `child_inverse`: each group's matrix, read as rows k and columns f * 2048 + j, is zero where k > j. `parent_inverse`: each group's matrix, read as rows k and columns f * 2048 + j, is zero where k > j. `root_inverse`: each group's matrix is zero below its diagonal.
All inputs are finite; a program needn't handle non-finite values.
Results may differ from a plain program's by a relative error of at most 0.02.
Values may be sent and summed in bfloat16 or wider, within the bound.
No kernel may reach another device: no remote copies, remote signals or barrier semaphores. Data moves between devices by JAX's collectives and lax.ppermute only.
A program may use at most 64 MiB of HBM per device.

v0:
```python
import functools

import jax
import jax.numpy as jnp
from jax import lax
from jax.experimental import pallas as pl
from jax.experimental.pallas import tpu as pltpu
from jax.sharding import PartitionSpec as P


LOW = 256
BF = jnp.bfloat16
F32 = jnp.float32
WHOLE = pl.BlockSpec(memory_space=pltpu.VMEM)


def call(kernel, outs, scratch, limit, cost, *args):
    return pl.pallas_call(
        kernel,
        out_shape=[jax.ShapeDtypeStruct(shape, dtype) for shape, dtype in outs],
        in_specs=[WHOLE] * len(args),
        out_specs=[WHOLE] * len(outs),
        scratch_shapes=scratch,
        compiler_params=pltpu.CompilerParams(vmem_limit_bytes=limit),
        cost_estimate=pl.CostEstimate(flops=cost[0], bytes_accessed=cost[1], transcendentals=0),
    )(*args)


def one_hot_rows(columns, low_ref):
    width = columns.shape[1]
    lane = lax.broadcasted_iota(jnp.int32, (LOW, width), 0)
    low_ref[...] = jnp.where(lane == (columns & (LOW - 1)), 1.0, 0.0).astype(BF)


def place_columns(values, columns, first, blocks, low_ref, stack_ref, put):
    rows = values.shape[0]
    high = columns // LOW
    together = stack_ref.shape[0] // rows
    for start in range(0, blocks, together):
        count = min(together, blocks - start)
        for j in range(count):
            here = jnp.where(high == first + start + j, 1.0, 0.0).astype(BF)
            stack_ref[j * rows : (j + 1) * rows, :] = values * here
        placed = lax.dot_general(
            stack_ref[: count * rows, :],
            low_ref[...],
            (((1,), (1,)), ((), ())),
            preferred_element_type=F32,
        )
        for j in range(count):
            put(start + j, placed[j * rows : (j + 1) * rows])


def shared_dot(pieces, weights, position, width, offset=0):
    total = None
    for k, piece in enumerate(pieces):
        first = pl.multiple_of(offset + (position ^ k) * width, width)
        part = jnp.dot(piece, weights[pl.ds(first, width), :], preferred_element_type=F32)
        total = part if total is None else total + part
    return total


def load_kernel(members, group, where, layer, *refs):
    (inverse, update, rhs, child_maps, parent_maps, root_rhs) = refs[:6]
    (inverse_v, update_v, partial, child_low, parent_low, columns, parent_columns) = refs[6:13]
    (placed_rhs, keep, lower_in, upper_in) = refs[13:17]
    rhs_v, child_maps_v, parent_maps_v, root_rhs_v, sems = refs[17:]
    pairs = (
        (child_maps, child_maps_v),
        (parent_maps, parent_maps_v),
        (root_rhs, root_rhs_v),
        (rhs, rhs_v),
        (inverse, inverse_v),
        (update, update_v),
    )
    copies = [pltpu.make_async_copy(a, b, sems.at[i]) for i, (a, b) in enumerate(pairs)]
    for copy in copies:
        copy.start()
    device = where()
    upper = device >= group
    copies[0].wait()
    columns[...] = child_maps_v[pl.ds(device // members, 1), :]
    one_hot_rows(columns[...], child_low)
    copies[1].wait()
    parent_columns[...] = parent_maps_v[pl.ds(device // group, 1), :]
    one_hot_rows(parent_columns[...], parent_low)
    copies[2].wait()
    width = root_rhs.shape[1]
    value = root_rhs_v[...].astype(F32)
    placed_rhs[:, :width] = jnp.where(upper, 0.0, value)
    placed_rhs[:, width:] = jnp.where(upper, value, 0.0)
    keep[:, :width] = jnp.ones((1, width), F32)
    above = jnp.where(upper, 1.0, 0.0)
    inside = jnp.where(layer() > 0, 1.0, 0.0)
    keep[:, width:] = jnp.full((1, width), above, F32)
    lower_in[...] = jnp.full((1, width), inside * (1.0 - above), F32)
    upper_in[...] = jnp.full((1, width), inside * above, F32)
    copies[3].wait()
    copies[4].wait()
    depth = rhs.shape[1]
    own = pl.multiple_of((device % members) * depth, depth)
    partial[...] = jnp.dot(
        rhs_v[...], inverse_v[pl.ds(own, depth), :], preferred_element_type=F32
    )
    copies[5].wait()


def child_kernel(pieces, members, group, where, *refs):
    piece_refs = refs[:pieces]
    partial, inverse, update, columns, low = refs[pieces : pieces + 5]
    sends = refs[pieces + 5 : pieces + 5 + group]
    terms, stack, summed = refs[pieces + 5 + group :]
    device = where()
    place, member = device % members, device % group
    solved = partial[...]
    for k, piece in enumerate(piece_refs, 1):
        depth = piece.shape[1]
        first = pl.multiple_of((place ^ k) * depth, depth)
        solved = solved + jnp.dot(
            piece[...], inverse[pl.ds(first, depth), :], preferred_element_type=F32
        )
    solved = solved.astype(BF)
    for start in range(0, update.shape[1], 512):
        terms[:, start : start + 512] = jnp.dot(
            solved, update[:, start : start + 512], preferred_element_type=F32
        ).astype(BF)

    def put(block, value):
        summed[:, block * LOW : (block + 1) * LOW] = value.astype(BF)

    place_columns(terms[...], columns[...], 0, summed.shape[1] // LOW, low, stack, put)
    width = sends[0].shape[1]
    for k, send in enumerate(sends):
        send[...] = summed[:, pl.ds(pl.multiple_of((member ^ k) * width, width), width)]


def child_root_kernel(parent_blocks, terms, columns, low, placed_ref, stack):
    def put(block, value):
        placed_ref[:, block * LOW : (block + 1) * LOW] = value.astype(BF)

    place_columns(
        terms[...], columns[...], parent_blocks, placed_ref.shape[1] // LOW, low, stack, put
    )


def parent_kernel(group, base, where, *refs):
    piece_refs = refs[:group]
    inverse, update, columns, low, child_root = refs[group : group + 5]
    sends = refs[group + 5 : 2 * group + 5]
    terms, stack, total = refs[2 * group + 5 :]
    member = where() % group
    rows, width = sends[0].shape[0], sends[0].shape[1] // 2
    here = slice(base, base + rows)
    solved = shared_dot([r[here, :] for r in piece_refs], inverse, member, piece_refs[0].shape[1])
    solved = solved.astype(BF)
    for start in range(0, update.shape[1], 512):
        terms[:, start : start + 512] = jnp.dot(
            solved, update[:, start : start + 512], preferred_element_type=F32
        ).astype(BF)

    def put(block, value):
        place = slice(block * LOW, (block + 1) * LOW)
        total[:, place] = (value + child_root[here, place].astype(F32)).astype(BF)

    place_columns(terms[...], columns[...], 0, total.shape[1] // LOW, low, stack, put)
    half = total.shape[1] // 2
    for k in range(group):
        first = pl.multiple_of((member ^ k) * width, width)
        second = pl.multiple_of(half + (member ^ k) * width, width)
        sends[k][:, :width] = total[:, pl.ds(first, width)]
        sends[k][:, width:] = total[:, pl.ds(second, width)]


def root_dot(group, where, piece_refs, inverse):
    member = where() % group
    width = piece_refs[0].shape[1] // 2
    lower = shared_dot([r[:, :width] for r in piece_refs], inverse, member, width)
    upper = shared_dot(
        [r[:, width:] for r in piece_refs], inverse, member, width, inverse.shape[0] // 2
    )
    return lower + upper


def first_root_kernel(group, where, *refs):
    piece_refs, (inverse, coupling, solved_ref, hand_ref) = refs[:group], refs[group:]
    solved = root_dot(group, where, piece_refs, inverse)
    solved_ref[...] = solved.astype(BF)
    hand_ref[...] = (coupling[...] * solved).astype(BF)


def second_root_kernel(group, where, *refs):
    piece_refs, (inverse, first_ref, out_ref) = refs[:group], refs[group:]
    solved = root_dot(group, where, piece_refs, inverse)
    rows = first_ref.shape[0]
    out_ref[:rows, :] = first_ref[...]
    out_ref[rows:, :] = solved.astype(BF)


def body(
    child_rhs,
    parent_rhs,
    root_rhs,
    child_inverse,
    child_update,
    parent_inverse,
    parent_update,
    root_inverse,
    coupling,
    child_map,
    parent_map,
):
    devices = lax.axis_size("front")
    layers = lax.axis_size("layer")
    members = devices // child_map.shape[0]
    group = devices // parent_map.shape[0]
    rows = child_rhs.shape[2]
    both = 2 * rows
    root_size = root_inverse.shape[1]
    parent_size = parent_inverse.shape[1]
    where = functools.partial(lax.axis_index, "front")
    layer = functools.partial(lax.axis_index, "layer")

    def trade(value, k):
        return lax.ppermute(value, "front", [(d, d ^ k) for d in range(devices)])

    rhs = child_rhs[0].reshape(both, child_rhs.shape[3])
    child_width = child_update.shape[2]
    parent_width = parent_update.shape[2]
    root_share = root_size // devices
    hbm = pl.BlockSpec(memory_space=pltpu.HBM)
    (inverse, update, partial, child_low, parent_low, columns, parent_columns, *masks) = pl.pallas_call(
        functools.partial(load_kernel, members, group, where, layer),
        name="load",
        out_shape=[
            jax.ShapeDtypeStruct(shape, dtype)
            for shape, dtype in (
                (child_inverse.shape[1:], BF),
                (child_update.shape[1:], BF),
                ((both, child_inverse.shape[2]), F32),
                ((LOW, child_width), BF),
                ((LOW, parent_width), BF),
                ((1, child_width), jnp.int32),
                ((1, parent_width), jnp.int32),
                ((both, 2 * root_share), F32),
                ((1, 2 * root_share), F32),
                ((1, root_share), F32),
                ((1, root_share), F32),
            )
        ],
        in_specs=[hbm] * 6,
        out_specs=[WHOLE] * 11,
        scratch_shapes=[
            pltpu.VMEM(rhs.shape, BF),
            pltpu.VMEM(child_map.shape, jnp.int32),
            pltpu.VMEM(parent_map.shape, jnp.int32),
            pltpu.VMEM((both, root_share), BF),
            pltpu.SemaphoreType.DMA((6,)),
        ],
        compiler_params=pltpu.CompilerParams(vmem_limit_bytes=8 << 20),
        cost_estimate=pl.CostEstimate(
            flops=both * child_inverse.size, bytes_accessed=child_inverse.size * 8, transcendentals=0
        ),
    )(
        *[
            pltpu.with_memory_space_constraint(value, pltpu.HBM)
            for value in (
                child_inverse[0],
                child_update[0],
                rhs,
                child_map,
                parent_map,
                root_rhs[0].reshape(both, root_share),
            )
        ]
    )
    placed_rhs, keep, lower_in, upper_in = masks
    share = parent_size // group
    *sends, terms = call(
        functools.partial(child_kernel, members - 1, members, group, where),
        [((both, share), BF)] * group + [((both, child_width), BF)],
        [pltpu.VMEM((4 * both, child_width), BF), pltpu.VMEM((both, parent_size), BF)],
        8 << 20,
        (both * 2 * child_inverse.size * 2, child_inverse.size * 4),
        *[trade(rhs, k) for k in range(1, members)],
        partial,
        inverse,
        update,
        columns,
        child_low,
    )
    (child_root,) = call(
        functools.partial(child_root_kernel, parent_size // LOW),
        [((both, root_size), BF)],
        [pltpu.VMEM((4 * both, child_width), BF)],
        8 << 20,
        (both * 2 * root_size * child_width, root_size * both * 4),
        terms,
        columns,
        child_low,
    )
    summed = sends[0].astype(F32)
    for k in range(1, group):
        summed = summed + trade(sends[k], k).astype(F32)
    parent_now = (
        parent_rhs[0].reshape(both, parent_rhs.shape[3]).astype(F32) - summed
    ).astype(BF)
    pieces = [parent_now] + [trade(parent_now, k) for k in range(1, group)]

    def parent_sends(block):
        return call(
            functools.partial(parent_kernel, group, block * rows, where),
            [((rows, 2 * root_share), BF)] * group,
            [
                pltpu.VMEM((rows, parent_width), BF),
                pltpu.VMEM((8 * rows, parent_width), BF),
                pltpu.VMEM((rows, root_size), BF),
            ],
            8 << 20,
            (rows * 2 * root_size * parent_width, parent_update.size * 4),
            *pieces,
            parent_inverse[0],
            parent_update[0],
            parent_columns,
            parent_low,
            child_root,
        )

    def group_sum(parts, block, after=()):
        arrived = [trade(parts[k], k) for k in range(1, group)]
        *_, first, arrived = lax.optimization_barrier((*after, parts[0], arrived))
        total = first.astype(F32)
        for value in arrived:
            total = total + value.astype(F32)
        return total - placed_rhs[block * rows : (block + 1) * rows]

    def gathered(now):
        return [now] + [trade(now, k) for k in range(1, group)]

    def crossed(part, narrow):
        return part + trade(narrow, group).astype(F32)

    root_cost = (rows * 2 * root_inverse.size, root_inverse.size * 2)
    part = group_sum(parent_sends(0), 0)
    now = (-crossed(part, part.astype(BF)) * keep).astype(BF)
    part = group_sum(parent_sends(1), 1, (now,))
    total = crossed(part, part.astype(BF))
    first_sol, outgoing = call(
        functools.partial(first_root_kernel, group, where),
        [((rows, root_share), BF), ((rows, root_share), BF)],
        [],
        4 << 20,
        root_cost,
        *gathered(now),
        root_inverse[0],
        coupling,
    )
    places = [(one, d) for one in range(layers) for d in range(devices)]
    same = [(g * devices + d, (g + 1) % layers * devices + d) for g, d in places]
    over = [(g * devices + d, (g + 1) % layers * devices + (d ^ group)) for g, d in places]
    incoming = lax.ppermute(outgoing, ("layer", "front"), same).astype(F32)
    beside = lax.ppermute(outgoing, ("layer", "front"), over).astype(F32)
    arrived = jnp.concatenate([incoming * lower_in + beside * upper_in, incoming * upper_in], 1)
    now = -(total + arrived) * keep
    (out,) = call(
        functools.partial(second_root_kernel, group, where),
        [((both, root_share), BF)],
        [],
        4 << 20,
        root_cost,
        *gathered(now.astype(BF)),
        root_inverse[0],
        first_sol,
    )
    return out.reshape(1, 2, rows, root_share)


def solution(mesh):
    placed = (
        P("layer", None, None, "front"),
        P("layer", None, None, "front"),
        P("layer", None, None, "front"),
        P("layer", None, "front"),
        P("layer", "front", None),
        P("layer", None, "front"),
        P("layer", "front", None),
        P("layer", None, "front"),
        P("layer", "front"),
        P(),
        P(),
    )

    return jax.shard_map(
        body, mesh=mesh, in_specs=placed, out_specs=P("layer", None, None, "front"), check_vma=False
    )
```

profile of v0, /device:TPU:0, one launch (start us, length us, event | category | flops | bytes accessed | tf_op | source)
XLA Modules:
  0.0 73.2 jit_solution(18404831631973326182)
XLA Ops:
  0.0 3.0 %collective-permute-start = (bf16[96,1024]{1,0:T(8,128)(2,1)}, bf16[96,1024]{1,0:T(8,128)(2,1)S(1)}, u32[]{:S(2)}, u32[]{:S(2)}) collective-permute-start(bf16[96,1024]{1,0:T(8,128)(2,1)} %bitcast.26), channel_id=1, source_target_pairs={{0,1},{1,0},{2,3},{3,2},{4,5},{5,4},{6,7},{7,6},{8,9},{9,8},{10,11... | collective-permute-start | bytes 589832 | tf_op jit(solution)/shard_map/ppermute | solution.py:224
  3.0 3.7 %load.1 = (bf16[2048,1024]{1,0:T(8,128)(2,1)S(1)}, bf16[1024,2048]{1,0:T(8,128)(2,1)S(1)}, f32[96,1024]{1,0:T(8,128)S(1)}, bf16[256,2048]{1,0:T(8,128)(2,1)S(1)}...) custom-call(bf16[2048,1024]{1,0:T(8,128)(2,1)} %bitcast.24, ...), custom_call_target="tpu_custom_call" | custom-call | flops 201326592 | bytes 16777216 | tf_op jit(solution)/shard_map/load/pallas_call | solution.py:231
  8.1 2.1 %shard_map.109 = (bf16[96,512]{1,0:T(8,128)(2,1)S(1)}, bf16[96,512]{1,0:T(8,128)(2,1)S(1)}, bf16[96,512]{1,0:T(8,128)(2,1)S(1)}, bf16[96,512]{1,0:T(8,128)(2,1)S(1)}, bf16[96,2048]{1,0:T(8,128)(2,1)S(1)}) custom-call(bf16[96,1024]{1,0:T(8,128)(2,1)S(1)} %collective-permute-done.refs_0_, f32[96,1024]{1,0:T(8,128)S(1)} %get-tuple-element.39.refs_1_, ...), custom_call_target="tpu_custom_call" | custom-call | flops 805306368 | bytes 8388608 | tf_op jit(solution)/shard_map/pallas_call | solution.py:18
  10.2 1.8 %collective-permute-start.1 = (bf16[96,512]{1,0:T(8,128)(2,1)S(1)}, bf16[96,512]{1,0:T(8,128)(2,1)S(1)}, u32[]{:S(2)}, u32[]{:S(2)}) collective-permute-start(bf16[96,512]{1,0:T(8,128)(2,1)S(1)} %get-tuple-element.45), channel_id=1, source_target_pairs={{0,1},{1,0},{2,3},{3,2},{4,5},{5,4},{6,7},{7,6},{8,9},{9,8},{10,11... | collective-permute-start | bytes 294920 | tf_op jit(solution)/shard_map/ppermute | solution.py:224
  12.0 1.6 %collective-permute-start.2 = (bf16[96,512]{1,0:T(8,128)(2,1)S(1)}, bf16[96,512]{1,0:T(8,128)(2,1)S(1)}, u32[]{:S(2)}, u32[]{:S(2)}) collective-permute-start(bf16[96,512]{1,0:T(8,128)(2,1)S(1)} %get-tuple-element.46), channel_id=1, source_target_pairs={{0,2},{1,3},{2,0},{3,1},{4,6},{5,7},{6,4},{7,5},{8,10},{9,11},{10,... | collective-permute-start | bytes 294920 | tf_op jit(solution)/shard_map/ppermute | solution.py:224
  16.7 2.4 %collective-permute-done.3 = bf16[96,512]{1,0:T(8,128)(2,1)S(1)} collective-permute-done((bf16[96,512]{1,0:T(8,128)(2,1)S(1)}, bf16[96,512]{1,0:T(8,128)(2,1)S(1)}, u32[]{:S(2)}, u32[]{:S(2)}) %collective-permute-start.3) | collective-permute-done | bytes 98336 | tf_op jit(solution)/shard_map/ppermute | solution.py:224
  21.2 1.5 %collective-permute-start.4 = (bf16[96,512]{1,0:T(8,128)(2,1)S(1)}, bf16[96,512]{1,0:T(8,128)(2,1)S(1)}, u32[]{:S(2)}, u32[]{:S(2)}) collective-permute-start(bf16[96,512]{1,0:T(8,128)(2,1)S(1)} %fusion.3.refs_0_), channel_id=1, source_target_pairs={{0,1},{1,0},{2,3},{3,2},{4,5},{5,4},{6,7},{7,6},{8,9},{9,8},{10,11... | collective-permute-start | bytes 294920 | tf_op jit(solution)/shard_map/ppermute | solution.py:224
  22.7 1.8 %shard_map.110.refs_8_ = bf16[96,4096]{1,0:T(8,128)(2,1)S(1)} custom-call(bf16[96,2048]{1,0:T(8,128)(2,1)S(1)} %get-tuple-element.50.terms, s32[1,2048]{1,0:T(1,128)S(1)} %get-tuple-element.42.refs_4_.columns, bf16[256,2048]{1,0:T(8,128)(2,1)S(1)} %get-tuple-element.43.refs_5_.low), custom_call_target="tpu_custom_call" | custom-call | flops 1610612736 | bytes 1572864 | tf_op jit(solution)/shard_map/pallas_call | solution.py:18
  25.9 2.4 %shard_map.111 = (bf16[48,1024]{1,0:T(8,128)(2,1)S(1)}, bf16[48,1024]{1,0:T(8,128)(2,1)S(1)}, bf16[48,1024]{1,0:T(8,128)(2,1)S(1)}, bf16[48,1024]{1,0:T(8,128)(2,1)S(1)}) custom-call(bf16[96,512]{1,0:T(8,128)(2,1)S(1)} %fusion.3.refs_0_, bf16[96,512]{1,0:T(8,128)(2,1)S(1)} %collective-permute-done.4.refs_1_, ...), custom_call_target="tpu_custom_call" | custom-call | flops 1207959552 | bytes 6291456 | tf_op jit(solution)/shard_map/pallas_call | solution.py:18
  28.3 1.6 %collective-permute-start.7 = (bf16[48,1024]{1,0:T(8,128)(2,1)S(1)}, bf16[48,1024]{1,0:T(8,128)(2,1)S(1)}, u32[]{:S(2)}, u32[]{:S(2)}) collective-permute-start(bf16[48,1024]{1,0:T(8,128)(2,1)S(1)} %get-tuple-element.52), channel_id=1, source_target_pairs={{0,1},{1,0},{2,3},{3,2},{4,5},{5,4},{6,7},{7,6},{8,9},{9,8},{10,11... | collective-permute-start | bytes 294920 | tf_op jit(solution)/shard_map/ppermute | solution.py:224
  30.3 1.5 %collective-permute-start.9 = (bf16[48,1024]{1,0:T(8,128)(2,1)S(1)}, bf16[48,1024]{1,0:T(8,128)(2,1)S(1)}, u32[]{:S(2)}, u32[]{:S(2)}) collective-permute-start(bf16[48,1024]{1,0:T(8,128)(2,1)S(1)} %get-tuple-element.54), channel_id=1, source_target_pairs={{0,3},{1,2},{2,1},{3,0},{4,7},{5,6},{6,5},{7,4},{8,11},{9,10},{10,... | collective-permute-start | bytes 294920 | tf_op jit(solution)/shard_map/ppermute | solution.py:224
  33.0 1.5 %collective-permute-done.8 = bf16[48,1024]{1,0:T(8,128)(2,1)S(1)} collective-permute-done((bf16[48,1024]{1,0:T(8,128)(2,1)S(1)}, bf16[48,1024]{1,0:T(8,128)(2,1)S(1)}, u32[]{:S(2)}, u32[]{:S(2)}) %collective-permute-start.8) | collective-permute-done | bytes 98336 | tf_op jit(solution)/shard_map/ppermute | solution.py:224
  34.5 2.4 %collective-permute-done.9 = bf16[48,1024]{1,0:T(8,128)(2,1)S(1)} collective-permute-done((bf16[48,1024]{1,0:T(8,128)(2,1)S(1)}, bf16[48,1024]{1,0:T(8,128)(2,1)S(1)}, u32[]{:S(2)}, u32[]{:S(2)}) %collective-permute-start.9) | collective-permute-done | bytes 98336 | tf_op jit(solution)/shard_map/ppermute | solution.py:224
  37.0 2.3 %collective-permute-start.10 = (bf16[48,1024]{1,0:T(8,128)(2,1)S(1)}, bf16[48,1024]{1,0:T(8,128)(2,1)S(1)}, u32[]{:S(2)}, u32[]{:S(2)}) collective-permute-start(bf16[48,1024]{1,0:T(8,128)(2,1)S(1)} %fusion.5), channel_id=1, source_target_pairs={{0,4},{1,5},{2,6},{3,7},{4,0},{5,1},{6,2},{7,3},{8,12},{9,13},{10,... | collective-permute-start | bytes 294920 | tf_op jit(solution)/shard_map/ppermute | solution.py:224
  39.3 2.4 %shard_map.112 = (bf16[48,1024]{1,0:T(8,128)(2,1)S(1)}, bf16[48,1024]{1,0:T(8,128)(2,1)S(1)}, bf16[48,1024]{1,0:T(8,128)(2,1)S(1)}, bf16[48,1024]{1,0:T(8,128)(2,1)S(1)}) custom-call(bf16[96,512]{1,0:T(8,128)(2,1)S(1)} %fusion.3.refs_0_, bf16[96,512]{1,0:T(8,128)(2,1)S(1)} %collective-permute-done.4.refs_1_, ...), custom_call_target="tpu_custom_call" | custom-call | flops 1207959552 | bytes 6291456 | tf_op jit(solution)/shard_map/pallas_call | solution.py:18
  43.6 1.7 %collective-permute-start.13 = (bf16[48,1024]{1,0:T(8,128)(2,1)S(1)}, bf16[48,1024]{1,0:T(8,128)(2,1)S(1)}, u32[]{:S(2)}, u32[]{:S(2)}) collective-permute-start(bf16[48,1024]{1,0:T(8,128)(2,1)S(1)} %get-tuple-element.64), channel_id=1, source_target_pairs={{0,3},{1,2},{2,1},{3,0},{4,7},{5,6},{6,5},{7,4},{8,11},{9,10},{10,... | collective-permute-start | bytes 294920 | tf_op jit(solution)/shard_map/ppermute | solution.py:224
  46.7 1.6 %collective-permute-start.16 = (bf16[48,1024]{1,0:T(8,128)(2,1)S(1)}, bf16[48,1024]{1,0:T(8,128)(2,1)S(1)}, u32[]{:S(2)}, u32[]{:S(2)}) collective-permute-start(bf16[48,1024]{1,0:T(8,128)(2,1)S(1)} %multiply_convert_fusion.refs_0_), channel_id=1, source_target_pairs={{0,2},{1,3},{2,0},{3,1},{4,6},{5,7},{6,4},{7,5},{8,10},{9,11},{10,... | collective-permute-start | bytes 294920 | tf_op jit(solution)/shard_map/ppermute | solution.py:224
  49.1 1.8 %collective-permute-done.17.refs_3_ = bf16[48,1024]{1,0:T(8,128)(2,1)S(1)} collective-permute-done((bf16[48,1024]{1,0:T(8,128)(2,1)S(1)}, bf16[48,1024]{1,0:T(8,128)(2,1)S(1)}, u32[]{:S(2)}, u32[]{:S(2)}) %collective-permute-start.17) | collective-permute-done | bytes 98336 | tf_op jit(solution)/shard_map/ppermute | solution.py:224
  53.8 1.7 %collective-permute-start.18 = (bf16[48,512]{1,0:T(8,128)(2,1)S(1)}, bf16[48,512]{1,0:T(8,128)(2,1)S(1)}, u32[]{:S(2)}, u32[]{:S(2)}) collective-permute-start(bf16[48,512]{1,0:T(8,128)(2,1)S(1)} %get-tuple-element.69), channel_id=1, source_target_pairs={{0,8},{1,9},{2,10},{3,11},{4,12},{5,13},{6,14},{7,15},{8,16},{9,17... | collective-permute-start | bytes 147464 | tf_op jit(solution)/shard_map/ppermute | solution.py:360
  55.6 2.4 %collective-permute-start.14 = (bf16[48,1024]{1,0:T(8,128)(2,1)S(1)}, bf16[48,1024]{1,0:T(8,128)(2,1)S(1)}, u32[]{:S(2)}, u32[]{:S(2)}) collective-permute-start(bf16[48,1024]{1,0:T(8,128)(2,1)S(1)} %fusion.6), channel_id=1, source_target_pairs={{0,4},{1,5},{2,6},{3,7},{4,0},{5,1},{6,2},{7,3},{8,12},{9,13},{10,... | collective-permute-start | bytes 294920 | tf_op jit(solution)/shard_map/ppermute | solution.py:224
  58.0 3.9 %collective-permute-done.19 = bf16[48,512]{1,0:T(8,128)(2,1)S(1)} collective-permute-done((bf16[48,512]{1,0:T(8,128)(2,1)S(1)}, bf16[48,512]{1,0:T(8,128)(2,1)S(1)}, u32[]{:S(2)}, u32[]{:S(2)}) %collective-permute-start.19) | collective-permute-done | bytes 49184 | tf_op jit(solution)/shard_map/ppermute | solution.py:361
  61.9 1.8 %collective-permute-done.14 = bf16[48,1024]{1,0:T(8,128)(2,1)S(1)} collective-permute-done((bf16[48,1024]{1,0:T(8,128)(2,1)S(1)}, bf16[48,1024]{1,0:T(8,128)(2,1)S(1)}, u32[]{:S(2)}, u32[]{:S(2)}) %collective-permute-start.14) | collective-permute-done | bytes 98336 | tf_op jit(solution)/shard_map/ppermute | solution.py:224
  64.0 2.2 %collective-permute-start.21 = (bf16[48,1024]{1,0:T(8,128)(2,1)S(1)}, bf16[48,1024]{1,0:T(8,128)(2,1)S(1)}, u32[]{:S(2)}, u32[]{:S(2)}) collective-permute-start(bf16[48,1024]{1,0:T(8,128)(2,1)S(1)} %fusion.2.refs_0_), channel_id=1, source_target_pairs={{0,2},{1,3},{2,0},{3,1},{4,6},{5,7},{6,4},{7,5},{8,10},{9,11},{10,... | collective-permute-start | bytes 294920 | tf_op jit(solution)/shard_map/ppermute | solution.py:224
  67.4 3.1 %collective-permute-done.22.refs_3_ = bf16[48,1024]{1,0:T(8,128)(2,1)S(1)} collective-permute-done((bf16[48,1024]{1,0:T(8,128)(2,1)S(1)}, bf16[48,1024]{1,0:T(8,128)(2,1)S(1)}, u32[]{:S(2)}, u32[]{:S(2)}) %collective-permute-start.22) | collective-permute-done | bytes 98336 | tf_op jit(solution)/shard_map/ppermute | solution.py:224
  (45 shorter events, 20.9 us)
Async XLA Ops:
  0.0 8.1 %collective-permute-start = (bf16[96,1024]{1,0:T(8,128)(2,1)}, bf16[96,1024]{1,0:T(8,128)(2,1)S(1)}, u32[]{:S(2)}, u32[]{:S(2)}) collective-permute-start(bf16[96,1024]{1,0:T(8,128)(2,1)} %bitcast.26), channel_id=1, source_target_pairs={{0,1},{1,0},{2,3},{3,2},{4,5},{5,4},{6,7},{7,6},{8,9},{9,8},{10,11... | collective-permute-start | bytes 589832 | tf_op jit(solution)/shard_map/ppermute | solution.py:224
  10.2 5.0 %collective-permute-start.1 = (bf16[96,512]{1,0:T(8,128)(2,1)S(1)}, bf16[96,512]{1,0:T(8,128)(2,1)S(1)}, u32[]{:S(2)}, u32[]{:S(2)}) collective-permute-start(bf16[96,512]{1,0:T(8,128)(2,1)S(1)} %get-tuple-element.45), channel_id=1, source_target_pairs={{0,1},{1,0},{2,3},{3,2},{4,5},{5,4},{6,7},{7,6},{8,9},{9,8},{10,11... | collective-permute-start | bytes 294920 | tf_op jit(solution)/shard_map/ppermute | solution.py:224
  12.0 4.7 %collective-permute-start.2 = (bf16[96,512]{1,0:T(8,128)(2,1)S(1)}, bf16[96,512]{1,0:T(8,128)(2,1)S(1)}, u32[]{:S(2)}, u32[]{:S(2)}) collective-permute-start(bf16[96,512]{1,0:T(8,128)(2,1)S(1)} %get-tuple-element.46), channel_id=1, source_target_pairs={{0,2},{1,3},{2,0},{3,1},{4,6},{5,7},{6,4},{7,5},{8,10},{9,11},{10,... | collective-permute-start | bytes 294920 | tf_op jit(solution)/shard_map/ppermute | solution.py:224
  13.6 5.5 %collective-permute-start.3 = (bf16[96,512]{1,0:T(8,128)(2,1)S(1)}, bf16[96,512]{1,0:T(8,128)(2,1)S(1)}, u32[]{:S(2)}, u32[]{:S(2)}) collective-permute-start(bf16[96,512]{1,0:T(8,128)(2,1)S(1)} %get-tuple-element.47), channel_id=1, source_target_pairs={{0,3},{1,2},{2,1},{3,0},{4,7},{5,6},{6,5},{7,4},{8,11},{9,10},{10,... | collective-permute-start | bytes 294920 | tf_op jit(solution)/shard_map/ppermute | solution.py:224
  19.2 5.6 %collective-permute-start.6 = (bf16[96,512]{1,0:T(8,128)(2,1)S(1)}, bf16[96,512]{1,0:T(8,128)(2,1)S(1)}, u32[]{:S(2)}, u32[]{:S(2)}) collective-permute-start(bf16[96,512]{1,0:T(8,128)(2,1)S(1)} %fusion.3.refs_0_), channel_id=1, source_target_pairs={{0,3},{1,2},{2,1},{3,0},{4,7},{5,6},{6,5},{7,4},{8,11},{9,10},{10,... | collective-permute-start | bytes 294920 | tf_op jit(solution)/shard_map/ppermute | solution.py:224
  20.3 4.6 %collective-permute-start.5 = (bf16[96,512]{1,0:T(8,128)(2,1)S(1)}, bf16[96,512]{1,0:T(8,128)(2,1)S(1)}, u32[]{:S(2)}, u32[]{:S(2)}) collective-permute-start(bf16[96,512]{1,0:T(8,128)(2,1)S(1)} %fusion.3.refs_0_), channel_id=1, source_target_pairs={{0,2},{1,3},{2,0},{3,1},{4,6},{5,7},{6,4},{7,5},{8,10},{9,11},{10,... | collective-permute-start | bytes 294920 | tf_op jit(solution)/shard_map/ppermute | solution.py:224
  21.2 4.6 %collective-permute-start.4 = (bf16[96,512]{1,0:T(8,128)(2,1)S(1)}, bf16[96,512]{1,0:T(8,128)(2,1)S(1)}, u32[]{:S(2)}, u32[]{:S(2)}) collective-permute-start(bf16[96,512]{1,0:T(8,128)(2,1)S(1)} %fusion.3.refs_0_), channel_id=1, source_target_pairs={{0,1},{1,0},{2,3},{3,2},{4,5},{5,4},{6,7},{7,6},{8,9},{9,8},{10,11... | collective-permute-start | bytes 294920 | tf_op jit(solution)/shard_map/ppermute | solution.py:224
  28.3 4.7 %collective-permute-start.7 = (bf16[48,1024]{1,0:T(8,128)(2,1)S(1)}, bf16[48,1024]{1,0:T(8,128)(2,1)S(1)}, u32[]{:S(2)}, u32[]{:S(2)}) collective-permute-start(bf16[48,1024]{1,0:T(8,128)(2,1)S(1)} %get-tuple-element.52), channel_id=1, source_target_pairs={{0,1},{1,0},{2,3},{3,2},{4,5},{5,4},{6,7},{7,6},{8,9},{9,8},{10,11... | collective-permute-start | bytes 294920 | tf_op jit(solution)/shard_map/ppermute | solution.py:224
  29.8 4.6 %collective-permute-start.8 = (bf16[48,1024]{1,0:T(8,128)(2,1)S(1)}, bf16[48,1024]{1,0:T(8,128)(2,1)S(1)}, u32[]{:S(2)}, u32[]{:S(2)}) collective-permute-start(bf16[48,1024]{1,0:T(8,128)(2,1)S(1)} %get-tuple-element.53), channel_id=1, source_target_pairs={{0,2},{1,3},{2,0},{3,1},{4,6},{5,7},{6,4},{7,5},{8,10},{9,11},{10,... | collective-permute-start | bytes 294920 | tf_op jit(solution)/shard_map/ppermute | solution.py:224
  30.3 6.6 %collective-permute-start.9 = (bf16[48,1024]{1,0:T(8,128)(2,1)S(1)}, bf16[48,1024]{1,0:T(8,128)(2,1)S(1)}, u32[]{:S(2)}, u32[]{:S(2)}) collective-permute-start(bf16[48,1024]{1,0:T(8,128)(2,1)S(1)} %get-tuple-element.54), channel_id=1, source_target_pairs={{0,3},{1,2},{2,1},{3,0},{4,7},{5,6},{6,5},{7,4},{8,11},{9,10},{10,... | collective-permute-start | bytes 294920 | tf_op jit(solution)/shard_map/ppermute | solution.py:224
  36.9 16.0 %copy-start = (bf16[1,4096,512]{2,1,0:T(8,128)(2,1)S(1)}, bf16[1,4096,512]{2,1,0:T(8,128)(2,1)}, u32[]{:S(2)}) copy-start(bf16[1,4096,512]{2,1,0:T(8,128)(2,1)} %param.18) | copy-start | bytes 12582916
  37.0 8.3 %collective-permute-start.10 = (bf16[48,1024]{1,0:T(8,128)(2,1)S(1)}, bf16[48,1024]{1,0:T(8,128)(2,1)S(1)}, u32[]{:S(2)}, u32[]{:S(2)}) collective-permute-start(bf16[48,1024]{1,0:T(8,128)(2,1)S(1)} %fusion.5), channel_id=1, source_target_pairs={{0,4},{1,5},{2,6},{3,7},{4,0},{5,1},{6,2},{7,3},{8,12},{9,13},{10,... | collective-permute-start | bytes 294920 | tf_op jit(solution)/shard_map/ppermute | solution.py:224
  41.7 6.6 %collective-permute-start.11 = (bf16[48,1024]{1,0:T(8,128)(2,1)S(1)}, bf16[48,1024]{1,0:T(8,128)(2,1)S(1)}, u32[]{:S(2)}, u32[]{:S(2)}) collective-permute-start(bf16[48,1024]{1,0:T(8,128)(2,1)S(1)} %get-tuple-element.62), channel_id=1, source_target_pairs={{0,1},{1,0},{2,3},{3,2},{4,5},{5,4},{6,7},{7,6},{8,9},{9,8},{10,11... | collective-permute-start | bytes 294920 | tf_op jit(solution)/shard_map/ppermute | solution.py:224
  43.2 5.8 %collective-permute-start.12 = (bf16[48,1024]{1,0:T(8,128)(2,1)S(1)}, bf16[48,1024]{1,0:T(8,128)(2,1)S(1)}, u32[]{:S(2)}, u32[]{:S(2)}) collective-permute-start(bf16[48,1024]{1,0:T(8,128)(2,1)S(1)} %get-tuple-element.63), channel_id=1, source_target_pairs={{0,2},{1,3},{2,0},{3,1},{4,6},{5,7},{6,4},{7,5},{8,10},{9,11},{10,... | collective-permute-start | bytes 294920 | tf_op jit(solution)/shard_map/ppermute | solution.py:224
  43.6 5.5 %collective-permute-start.13 = (bf16[48,1024]{1,0:T(8,128)(2,1)S(1)}, bf16[48,1024]{1,0:T(8,128)(2,1)S(1)}, u32[]{:S(2)}, u32[]{:S(2)}) collective-permute-start(bf16[48,1024]{1,0:T(8,128)(2,1)S(1)} %get-tuple-element.64), channel_id=1, source_target_pairs={{0,3},{1,2},{2,1},{3,0},{4,7},{5,6},{6,5},{7,4},{8,11},{9,10},{10,... | collective-permute-start | bytes 294920 | tf_op jit(solution)/shard_map/ppermute | solution.py:224
  45.4 5.6 %collective-permute-start.17 = (bf16[48,1024]{1,0:T(8,128)(2,1)S(1)}, bf16[48,1024]{1,0:T(8,128)(2,1)S(1)}, u32[]{:S(2)}, u32[]{:S(2)}) collective-permute-start(bf16[48,1024]{1,0:T(8,128)(2,1)S(1)} %multiply_convert_fusion.refs_0_), channel_id=1, source_target_pairs={{0,3},{1,2},{2,1},{3,0},{4,7},{5,6},{6,5},{7,4},{8,11},{9,10},{10,... | collective-permute-start | bytes 294920 | tf_op jit(solution)/shard_map/ppermute | solution.py:224
  46.7 5.2 %collective-permute-start.16 = (bf16[48,1024]{1,0:T(8,128)(2,1)S(1)}, bf16[48,1024]{1,0:T(8,128)(2,1)S(1)}, u32[]{:S(2)}, u32[]{:S(2)}) collective-permute-start(bf16[48,1024]{1,0:T(8,128)(2,1)S(1)} %multiply_convert_fusion.refs_0_), channel_id=1, source_target_pairs={{0,2},{1,3},{2,0},{3,1},{4,6},{5,7},{6,4},{7,5},{8,10},{9,11},{10,... | collective-permute-start | bytes 294920 | tf_op jit(solution)/shard_map/ppermute | solution.py:224
  48.3 4.6 %collective-permute-start.15 = (bf16[48,1024]{1,0:T(8,128)(2,1)S(1)}, bf16[48,1024]{1,0:T(8,128)(2,1)S(1)}, u32[]{:S(2)}, u32[]{:S(2)}) collective-permute-start(bf16[48,1024]{1,0:T(8,128)(2,1)S(1)} %multiply_convert_fusion.refs_0_), channel_id=1, source_target_pairs={{0,1},{1,0},{2,3},{3,2},{4,5},{5,4},{6,7},{7,6},{8,9},{9,8},{10,11... | collective-permute-start | bytes 294920 | tf_op jit(solution)/shard_map/ppermute | solution.py:224
  53.8 8.2 %collective-permute-start.19 = (bf16[48,512]{1,0:T(8,128)(2,1)S(1)}, bf16[48,512]{1,0:T(8,128)(2,1)S(1)}, u32[]{:S(2)}, u32[]{:S(2)}) collective-permute-start(bf16[48,512]{1,0:T(8,128)(2,1)S(1)} %get-tuple-element.69), channel_id=1, source_target_pairs={{0,12},{1,13},{2,14},{3,15},{4,8},{5,9},{6,10},{7,11},{8,20},{9,21... | collective-permute-start | bytes 147464 | tf_op jit(solution)/shard_map/ppermute | solution.py:361
  53.8 8.1 %collective-permute-start.18 = (bf16[48,512]{1,0:T(8,128)(2,1)S(1)}, bf16[48,512]{1,0:T(8,128)(2,1)S(1)}, u32[]{:S(2)}, u32[]{:S(2)}) collective-permute-start(bf16[48,512]{1,0:T(8,128)(2,1)S(1)} %get-tuple-element.69), channel_id=1, source_target_pairs={{0,8},{1,9},{2,10},{3,11},{4,12},{5,13},{6,14},{7,15},{8,16},{9,17... | collective-permute-start | bytes 147464 | tf_op jit(solution)/shard_map/ppermute | solution.py:360
  55.6 8.2 %collective-permute-start.14 = (bf16[48,1024]{1,0:T(8,128)(2,1)S(1)}, bf16[48,1024]{1,0:T(8,128)(2,1)S(1)}, u32[]{:S(2)}, u32[]{:S(2)}) collective-permute-start(bf16[48,1024]{1,0:T(8,128)(2,1)S(1)} %fusion.6), channel_id=1, source_target_pairs={{0,4},{1,5},{2,6},{3,7},{4,0},{5,1},{6,2},{7,3},{8,12},{9,13},{10,... | collective-permute-start | bytes 294920 | tf_op jit(solution)/shard_map/ppermute | solution.py:224
  63.9 6.6 %collective-permute-start.22 = (bf16[48,1024]{1,0:T(8,128)(2,1)S(1)}, bf16[48,1024]{1,0:T(8,128)(2,1)S(1)}, u32[]{:S(2)}, u32[]{:S(2)}) collective-permute-start(bf16[48,1024]{1,0:T(8,128)(2,1)S(1)} %fusion.2.refs_0_), channel_id=1, source_target_pairs={{0,3},{1,2},{2,1},{3,0},{4,7},{5,6},{6,5},{7,4},{8,11},{9,10},{10,... | collective-permute-start | bytes 294920 | tf_op jit(solution)/shard_map/ppermute | solution.py:224
  64.0 6.5 %collective-permute-start.21 = (bf16[48,1024]{1,0:T(8,128)(2,1)S(1)}, bf16[48,1024]{1,0:T(8,128)(2,1)S(1)}, u32[]{:S(2)}, u32[]{:S(2)}) collective-permute-start(bf16[48,1024]{1,0:T(8,128)(2,1)S(1)} %fusion.2.refs_0_), channel_id=1, source_target_pairs={{0,2},{1,3},{2,0},{3,1},{4,6},{5,7},{6,4},{7,5},{8,10},{9,11},{10,... | collective-permute-start | bytes 294920 | tf_op jit(solution)/shard_map/ppermute | solution.py:224
  66.2 5.5 %collective-permute-start.20 = (bf16[48,1024]{1,0:T(8,128)(2,1)S(1)}, bf16[48,1024]{1,0:T(8,128)(2,1)S(1)}, u32[]{:S(2)}, u32[]{:S(2)}) collective-permute-start(bf16[48,1024]{1,0:T(8,128)(2,1)S(1)} %fusion.2.refs_0_), channel_id=1, source_target_pairs={{0,1},{1,0},{2,3},{3,2},{4,5},{5,4},{6,7},{7,6},{8,9},{9,8},{10,11... | collective-permute-start | bytes 294920 | tf_op jit(solution)/shard_map/ppermute | solution.py:224
  (4 other events, 58.4 us)
where the time goes:
time: 73.4 us; the launch traced here: 73.2 us
  starting transfers between devices  30.8 us (42%)
  waiting for transfers between devices  27.1 us (37%)
  Pallas kernels  14.8 us (20%)
    ppermute x21, starting transfers between devices, trade(): return lax.ppermute(value, 'front', [(d, d ^ k) for d in range(devices)])  29 us
    ppermute x21, waiting for transfers between devices, trade(): return lax.ppermute(value, 'front', [(d, d ^ k) for d in range(devices)])  23.2 us
    pallas_call x6, Pallas kernels, call(): pl.pallas_call(kernel, out_shape=[jax.ShapeDtypeStruct(shape, dtype) for...  11.1 us
    ppermute x1, waiting for transfers between devices, body(): beside = lax.ppermute(outgoing, ('layer', 'front'), over).astype(F32)  3.91 us
    pallas_call x1, Pallas kernels, body(): pl.pallas_call(functools.partial(load_kernel, members, group, where, laye...  3.71 us
    ppermute x1, starting transfers between devices, body(): incoming = lax.ppermute(outgoing, ('layer', 'front'), same).astype(F32)  1.69 us
  transfers between devices with their start and end apart: 23, of which 18 were waited for; matrix products, arithmetic and copies ran while one was open for 0% of the time, Pallas kernels for 11%

commit v1 on v0

--- a/solution.py
+++ b/solution.py
@@ -49,15 +49,6 @@
         )
         for j in range(count):
             put(start + j, placed[j * rows : (j + 1) * rows])
-
-
-def shared_dot(pieces, weights, position, width, offset=0):
-    total = None
-    for k, piece in enumerate(pieces):
-        first = pl.multiple_of(offset + (position ^ k) * width, width)
-        part = jnp.dot(piece, weights[pl.ds(first, width), :], preferred_element_type=F32)
-        total = part if total is None else total + part
-    return total
 
 
 def load_kernel(members, group, where, layer, *refs):
@@ -105,19 +96,19 @@
     copies[5].wait()
 
 
-def child_kernel(pieces, members, group, where, *refs):
+def child_kernel(pieces, base, members, group, where, *refs):
     piece_refs = refs[:pieces]
-    partial, inverse, update, columns, low = refs[pieces : pieces + 5]
-    sends = refs[pieces + 5 : pieces + 5 + group]
-    terms, stack, summed = refs[pieces + 5 + group :]
+    partial, inverse, update, columns, low, rhs = refs[pieces : pieces + 6]
+    out, terms, stack, summed = refs[pieces + 6 :]
     device = where()
     place, member = device % members, device % group
-    solved = partial[...]
+    here = slice(base, base + out.shape[0])
+    solved = partial[here, :]
     for k, piece in enumerate(piece_refs, 1):
         depth = piece.shape[1]
         first = pl.multiple_of((place ^ k) * depth, depth)
         solved = solved + jnp.dot(
-            piece[...], inverse[pl.ds(first, depth), :], preferred_element_type=F32
+            piece[here, :], inverse[pl.ds(first, depth), :], preferred_element_type=F32
         )
     solved = solved.astype(BF)
     for start in range(0, update.shape[1], 512):
@@ -126,12 +117,13 @@
         ).astype(BF)
 
     def put(block, value):
-        summed[:, block * LOW : (block + 1) * LOW] = value.astype(BF)
+        summed[:, block * LOW : (block + 1) * LOW] = value
 
     place_columns(terms[...], columns[...], 0, summed.shape[1] // LOW, low, stack, put)
-    width = sends[0].shape[1]
-    for k, send in enumerate(sends):
-        send[...] = summed[:, pl.ds(pl.multiple_of((member ^ k) * width, width), width)]
+    width = rhs.shape[1]
+    own = pl.ds(pl.multiple_of(member * width, width), width)
+    summed[:, own] = summed[:, own] - rhs[here, :].astype(F32)
+    out[...] = summed[...].astype(BF)
 
 
 def child_root_kernel(parent_blocks, terms, columns, low, placed_ref, stack):
@@ -143,16 +135,13 @@
     )
 
 
-def parent_kernel(group, base, where, *refs):
-    piece_refs = refs[:group]
-    inverse, update, columns, low, child_root = refs[group : group + 5]
-    sends = refs[group + 5 : 2 * group + 5]
-    terms, stack, total = refs[2 * group + 5 :]
+def parent_kernel(group, where, *refs):
+    now, inverse, update, columns, low, child_root = refs[:6]
+    sends = refs[6 : 6 + group]
+    terms, stack, total = refs[6 + group :]
     member = where() % group
-    rows, width = sends[0].shape[0], sends[0].shape[1] // 2
-    here = slice(base, base + rows)
-    solved = shared_dot([r[here, :] for r in piece_refs], inverse, member, piece_refs[0].shape[1])
-    solved = solved.astype(BF)
+    width = sends[0].shape[1] // 2
+    solved = jnp.dot(now[...], inverse[...], preferred_element_type=F32).astype(BF)
     for start in range(0, update.shape[1], 512):
         terms[:, start : start + 512] = jnp.dot(
             solved, update[:, start : start + 512], preferred_element_type=F32
@@ -160,7 +149,7 @@
 
     def put(block, value):
         place = slice(block * LOW, (block + 1) * LOW)
-        total[:, place] = (value + child_root[here, place].astype(F32)).astype(BF)
+        total[:, place] = (value + child_root[:, place].astype(F32)).astype(BF)
 
     place_columns(terms[...], columns[...], 0, total.shape[1] // LOW, low, stack, put)
     half = total.shape[1] // 2
@@ -171,26 +160,38 @@
         sends[k][:, width:] = total[:, pl.ds(second, width)]
 
 
-def root_dot(group, where, piece_refs, inverse):
+def root_dot(group, where, members, piece_refs, inverse):
     member = where() % group
-    width = piece_refs[0].shape[1] // 2
-    lower = shared_dot([r[:, :width] for r in piece_refs], inverse, member, width)
-    upper = shared_dot(
-        [r[:, width:] for r in piece_refs], inverse, member, width, inverse.shape[0] // 2
-    )
-    return lower + upper
-
-
-def first_root_kernel(group, where, *refs):
-    piece_refs, (inverse, coupling, solved_ref, hand_ref) = refs[:group], refs[group:]
-    solved = root_dot(group, where, piece_refs, inverse)
+    half = inverse.shape[0] // 2
+    total = None
+    for k, piece in zip(members, piece_refs):
+        width = piece.shape[1] // 2
+        for part in range(2):
+            first = pl.multiple_of(part * half + (member ^ k) * width, width)
+            value = jnp.dot(
+                piece[:, part * width : (part + 1) * width],
+                inverse[pl.ds(first, width), :],
+                preferred_element_type=F32,
+            )
+            total = value if total is None else total + value
+    return total
+
+
+def early_root_kernel(group, where, members, *refs):
+    *piece_refs, inverse, total = refs
+    total[...] = root_dot(group, where, members, piece_refs, inverse)
+
+
+def first_root_kernel(group, where, members, *refs):
+    *piece_refs, inverse, early, coupling, solved_ref, hand_ref = refs
+    solved = early[...] + root_dot(group, where, members, piece_refs, inverse)
     solved_ref[...] = solved.astype(BF)
     hand_ref[...] = (coupling[...] * solved).astype(BF)
 
 
-def second_root_kernel(group, where, *refs):
-    piece_refs, (inverse, first_ref, out_ref) = refs[:group], refs[group:]
-    solved = root_dot(group, where, piece_refs, inverse)
+def second_root_kernel(group, where, members, *refs):
+    *piece_refs, inverse, early, first_ref, out_ref = refs
+    solved = early[...] + root_dot(group, where, members, piece_refs, inverse)
     rows = first_ref.shape[0]
     out_ref[:rows, :] = first_ref[...]
     out_ref[rows:, :] = solved.astype(BF)
@@ -274,41 +275,43 @@
         ]
     )
     placed_rhs, keep, lower_in, upper_in = masks
-    share = parent_size // group
-    *sends, terms = call(
-        functools.partial(child_kernel, members - 1, members, group, where),
-        [((both, share), BF)] * group + [((both, child_width), BF)],
-        [pltpu.VMEM((4 * both, child_width), BF), pltpu.VMEM((both, parent_size), BF)],
-        8 << 20,
-        (both * 2 * child_inverse.size * 2, child_inverse.size * 4),
-        *[trade(rhs, k) for k in range(1, members)],
-        partial,
-        inverse,
-        update,
-        columns,
-        child_low,
-    )
-    (child_root,) = call(
-        functools.partial(child_root_kernel, parent_size // LOW),
-        [((both, root_size), BF)],
-        [pltpu.VMEM((4 * both, child_width), BF)],
-        8 << 20,
-        (both * 2 * root_size * child_width, root_size * both * 4),
-        terms,
-        columns,
-        child_low,
-    )
-    summed = sends[0].astype(F32)
-    for k in range(1, group):
-        summed = summed + trade(sends[k], k).astype(F32)
-    parent_now = (
-        parent_rhs[0].reshape(both, parent_rhs.shape[3]).astype(F32) - summed
-    ).astype(BF)
-    pieces = [parent_now] + [trade(parent_now, k) for k in range(1, group)]
+    own_rhs = parent_rhs[0].reshape(both, parent_rhs.shape[3])
+
+    pieces = [trade(rhs, k) for k in range(1, members)]
+
+    def child_part(block):
+        return call(
+            functools.partial(child_kernel, members - 1, block * rows, members, group, where),
+            [((rows, parent_size), BF), ((rows, child_width), BF)],
+            [pltpu.VMEM((8 * rows, child_width), BF), pltpu.VMEM((rows, parent_size), F32)],
+            8 << 20,
+            (rows * 2 * child_inverse.size * 2, child_inverse.size * 4),
+            *pieces,
+            partial,
+            inverse,
+            update,
+            columns,
+            child_low,
+            own_rhs,
+        )
 
     def parent_sends(block):
+        part, terms = child_part(block)
+        (child_root,) = call(
+            functools.partial(child_root_kernel, parent_size // LOW),
+            [((rows, root_size), BF)],
+            [pltpu.VMEM((8 * rows, child_width), BF)],
+            8 << 20,
+            (rows * 2 * root_size * child_width, root_size * rows * 4),
+            terms,
+            columns,
+            child_low,
+        )
+        steps = [1 << bit for bit in range((group - 1).bit_length())]
+        for step in reversed(steps) if block else steps:
+            part = (part.astype(F32) + trade(part, step).astype(F32)).astype(BF)
         return call(
-            functools.partial(parent_kernel, group, block * rows, where),
+            functools.partial(parent_kernel, group, where),
             [((rows, 2 * root_share), BF)] * group,
             [
                 pltpu.VMEM((rows, parent_width), BF),
@@ -317,7 +320,7 @@
             ],
             8 << 20,
             (rows * 2 * root_size * parent_width, parent_update.size * 4),
-            *pieces,
+            -part,
             parent_inverse[0],
             parent_update[0],
             parent_columns,
@@ -327,31 +330,47 @@
 
     def group_sum(parts, block, after=()):
         arrived = [trade(parts[k], k) for k in range(1, group)]
-        *_, first, arrived = lax.optimization_barrier((*after, parts[0], arrived))
-        total = first.astype(F32)
+        own = parts[0]
+        if after:
+            *_, own = lax.optimization_barrier((*after, own))
+        total = own.astype(F32) - placed_rhs[block * rows : (block + 1) * rows]
+        if after:
+            total, arrived = lax.optimization_barrier((total, arrived))
         for value in arrived:
             total = total + value.astype(F32)
-        return total - placed_rhs[block * rows : (block + 1) * rows]
+        return total
+
+    early_ones = (0, group - 1)
+    late_ones = tuple(range(1, group - 1))
 
     def gathered(now):
-        return [now] + [trade(now, k) for k in range(1, group)]
+        pieces = [now] + [trade(now, k) for k in range(1, group)]
+        (early,) = call(
+            functools.partial(early_root_kernel, group, where, early_ones),
+            [((rows, root_share), F32)],
+            [],
+            4 << 20,
+            root_cost,
+            *[pieces[k] for k in early_ones],
+            root_inverse[0],
+        )
+        return [pieces[k] for k in late_ones] + [root_inverse[0], early]
 
     def crossed(part, narrow):
         return part + trade(narrow, group).astype(F32)
 
-    root_cost = (rows * 2 * root_inverse.size, root_inverse.size * 2)
+    root_cost = (rows * root_inverse.size, root_inverse.size)
     part = group_sum(parent_sends(0), 0)
     now = (-crossed(part, part.astype(BF)) * keep).astype(BF)
     part = group_sum(parent_sends(1), 1, (now,))
     total = crossed(part, part.astype(BF))
     first_sol, outgoing = call(
-        functools.partial(first_root_kernel, group, where),
+        functools.partial(first_root_kernel, group, where, late_ones),
         [((rows, root_share), BF), ((rows, root_share), BF)],
         [],
         4 << 20,
         root_cost,
         *gathered(now),
-        root_inverse[0],
         coupling,
     )
     places = [(one, d) for one in range(layers) for d in range(devices)]
@@ -362,13 +381,12 @@
     arrived = jnp.concatenate([incoming * lower_in + beside * upper_in, incoming * upper_in], 1)
     now = -(total + arrived) * keep
     (out,) = call(
-        functools.partial(second_root_kernel, group, where),
+        functools.partial(second_root_kernel, group, where, late_ones),
         [((both, root_share), BF)],
         [],
         4 << 20,
         root_cost,
         *gathered(now.astype(BF)),
-        root_inverse[0],
         first_sol,
     )
     return out.reshape(1, 2, rows, root_share)

time: 73.4 us -> 70.1 us (0.955)
  waiting for transfers between devices: 27.1 us -> 23.9 us
  starting transfers between devices: 30.8 us -> 28.6 us
  Pallas kernels: 14.8 us -> 16.6 us
    ppermute x21 -> x19, waiting for transfers between devices: 23.2 us -> 20.3 us  [trade(): return lax.ppermute(value, 'front', [(d, d ^ k) for d in range(devices)])]
    ppermute x21 -> x19, starting transfers between devices: 29 us -> 26.9 us  [trade(): return lax.ppermute(value, 'front', [(d, d ^ k) for d in range(devices)])]
    pallas_call x6 -> x10, Pallas kernels: 11.1 us -> 12.9 us  [call(): pl.pallas_call(kernel, out_shape=[jax.ShapeDtypeStruct(shape, dtype) for...]
  transfers between devices with their start and end apart: 23 -> 21, of which waited for: 18 -> 14; matrix products, arithmetic and copies ran while one was open for 0% -> 1% of each run, Pallas kernels for 11% -> 19%
where the time goes in v1:
time: 70.1 us; the launch traced here: 69.9 us
  starting transfers between devices  28.6 us (41%)
  waiting for transfers between devices  23.9 us (34%)
  Pallas kernels  16.6 us (24%)
    ppermute x19, starting transfers between devices, trade(): return lax.ppermute(value, 'front', [(d, d ^ k) for d in range(devices)])  26.9 us
    ppermute x19, waiting for transfers between devices, trade(): return lax.ppermute(value, 'front', [(d, d ^ k) for d in range(devices)])  20.3 us
    pallas_call x10, Pallas kernels, call(): pl.pallas_call(kernel, out_shape=[jax.ShapeDtypeStruct(shape, dtype) for...  12.9 us
    pallas_call x1, Pallas kernels, body(): pl.pallas_call(functools.partial(load_kernel, members, group, where, laye...  3.74 us
    ppermute x1, waiting for transfers between devices, body(): beside = lax.ppermute(outgoing, ('layer', 'front'), over).astype(F32)  3.62 us
    ppermute x1, starting transfers between devices, body(): incoming = lax.ppermute(outgoing, ('layer', 'front'), same).astype(F32)  1.62 us
  transfers between devices with their start and end apart: 21, of which 14 were waited for; matrix products, arithmetic and copies ran while one was open for 1% of the time, Pallas kernels for 19%

profile of v1, /device:TPU:0, one launch (start us, length us, event | category | flops | bytes accessed | tf_op | source)
XLA Modules:
  0.0 69.9 jit_solution(7268886174642876663)
XLA Ops:
  0.0 3.0 %collective-permute-start = (bf16[96,1024]{1,0:T(8,128)(2,1)}, bf16[96,1024]{1,0:T(8,128)(2,1)S(1)}, u32[]{:S(2)}, u32[]{:S(2)}) collective-permute-start(bf16[96,1024]{1,0:T(8,128)(2,1)} %bitcast.28), channel_id=1, source_target_pairs={{0,1},{1,0},{2,3},{3,2},{4,5},{5,4},{6,7},{7,6},{8,9},{9,8},{10,11... | collective-permute-start | bytes 589832 | tf_op jit(solution)/shard_map/ppermute | solution.py:225
  3.0 3.7 %load.1 = (bf16[2048,1024]{1,0:T(8,128)(2,1)S(1)}, bf16[1024,2048]{1,0:T(8,128)(2,1)S(1)}, f32[96,1024]{1,0:T(8,128)S(1)}, bf16[256,2048]{1,0:T(8,128)(2,1)S(1)}...) custom-call(bf16[2048,1024]{1,0:T(8,128)(2,1)} %bitcast.26, ...), custom_call_target="tpu_custom_call" | custom-call | flops 201326592 | bytes 16777216 | tf_op jit(solution)/shard_map/load/pallas_call | solution.py:232
  8.1 1.8 %shard_map.109 = (bf16[48,2048]{1,0:T(8,128)(2,1)S(1)}, bf16[48,2048]{1,0:T(8,128)(2,1)S(1)}) custom-call(bf16[96,1024]{1,0:T(8,128)(2,1)S(1)} %collective-permute-done.refs_0_, f32[96,1024]{1,0:T(8,128)S(1)} %get-tuple-element.35.refs_1_, bf16[2048,1024]{1,0:T(8,128)(2,1)S(1)} %get-tuple-element.36.refs_2_, ...), custom_call_target="tpu_custom_call" | custom-call | flops 402653184 | bytes 8388608 | tf_op jit(solution)/shard_map/pallas_call | solution.py:18
  9.9 1.8 %collective-permute-start.1 = (bf16[48,2048]{1,0:T(8,128)(2,1)S(1)}, bf16[48,2048]{1,0:T(8,128)(2,1)S(1)}, u32[]{:S(2)}, u32[]{:S(2)}) collective-permute-start(bf16[48,2048]{1,0:T(8,128)(2,1)S(1)} %get-tuple-element.40), channel_id=1, source_target_pairs={{0,1},{1,0},{2,3},{3,2},{4,5},{5,4},{6,7},{7,6},{8,9},{9,8},{10,11... | collective-permute-start | bytes 589832 | tf_op jit(solution)/shard_map/ppermute | solution.py:225
  11.7 1.8 %shard_map.112 = (bf16[48,2048]{1,0:T(8,128)(2,1)S(1)}, bf16[48,2048]{1,0:T(8,128)(2,1)S(1)}) custom-call(bf16[96,1024]{1,0:T(8,128)(2,1)S(1)} %collective-permute-done.refs_0_, f32[96,1024]{1,0:T(8,128)S(1)} %get-tuple-element.35.refs_1_, bf16[2048,1024]{1,0:T(8,128)(2,1)S(1)} %get-tuple-element.36.refs_2_, ...), custom_call_target="tpu_custom_call" | custom-call | flops 402653184 | bytes 8388608 | tf_op jit(solution)/shard_map/pallas_call | solution.py:18
  13.5 1.6 %collective-permute-start.7 = (bf16[48,2048]{1,0:T(8,128)(2,1)S(1)}, bf16[48,2048]{1,0:T(8,128)(2,1)S(1)}, u32[]{:S(2)}, u32[]{:S(2)}) collective-permute-start(bf16[48,2048]{1,0:T(8,128)(2,1)S(1)} %get-tuple-element.50), channel_id=1, source_target_pairs={{0,2},{1,3},{2,0},{3,1},{4,6},{5,7},{6,4},{7,5},{8,10},{9,11},{10,... | collective-permute-start | bytes 589832 | tf_op jit(solution)/shard_map/ppermute | solution.py:225
  17.7 2.6 %collective-permute-done.7 = bf16[48,2048]{1,0:T(8,128)(2,1)S(1)} collective-permute-done((bf16[48,2048]{1,0:T(8,128)(2,1)S(1)}, bf16[48,2048]{1,0:T(8,128)(2,1)S(1)}, u32[]{:S(2)}, u32[]{:S(2)}) %collective-permute-start.7) | collective-permute-done | bytes 196640 | tf_op jit(solution)/shard_map/ppermute | solution.py:225
  20.5 2.9 %collective-permute-done.2 = bf16[48,2048]{1,0:T(8,128)(2,1)S(1)} collective-permute-done((bf16[48,2048]{1,0:T(8,128)(2,1)S(1)}, bf16[48,2048]{1,0:T(8,128)(2,1)S(1)}, u32[]{:S(2)}, u32[]{:S(2)}) %collective-permute-start.2) | collective-permute-done | bytes 196640 | tf_op jit(solution)/shard_map/ppermute | solution.py:225
  23.5 2.4 %shard_map.111 = (bf16[48,1024]{1,0:T(8,128)(2,1)S(1)}, bf16[48,1024]{1,0:T(8,128)(2,1)S(1)}, bf16[48,1024]{1,0:T(8,128)(2,1)S(1)}, bf16[48,1024]{1,0:T(8,128)(2,1)S(1)}) custom-call(bf16[48,2048]{1,0:T(8,128)(2,1)S(1)} %fusion.refs_0_, bf16[2048,512]{1,0:T(8,128)(2,1)S(1)} %bitcast.18, bf16[512,3072]{1,0:T(8,128)(2,1)S(1)} %bitcast.16, ...), custom_call_target="tpu_custom_call" | custom-call | flops 1207959552 | bytes 6291456 | tf_op jit(solution)/shard_map/pallas_call | solution.py:18
  26.4 1.7 %collective-permute-start.4 = (bf16[48,1024]{1,0:T(8,128)(2,1)S(1)}, bf16[48,1024]{1,0:T(8,128)(2,1)S(1)}, u32[]{:S(2)}, u32[]{:S(2)}) collective-permute-start(bf16[48,1024]{1,0:T(8,128)(2,1)S(1)} %get-tuple-element.47), channel_id=1, source_target_pairs={{0,2},{1,3},{2,0},{3,1},{4,6},{5,7},{6,4},{7,5},{8,10},{9,11},{10,... | collective-permute-start | bytes 294920 | tf_op jit(solution)/shard_map/ppermute | solution.py:225
  28.1 1.4 %collective-permute-start.5 = (bf16[48,1024]{1,0:T(8,128)(2,1)S(1)}, bf16[48,1024]{1,0:T(8,128)(2,1)S(1)}, u32[]{:S(2)}, u32[]{:S(2)}) collective-permute-start(bf16[48,1024]{1,0:T(8,128)(2,1)S(1)} %get-tuple-element.48), channel_id=1, source_target_pairs={{0,3},{1,2},{2,1},{3,0},{4,7},{5,6},{6,5},{7,4},{8,11},{9,10},{10,... | collective-permute-start | bytes 294920 | tf_op jit(solution)/shard_map/ppermute | solution.py:225
  29.5 2.1 %collective-permute-done.3 = bf16[48,1024]{1,0:T(8,128)(2,1)S(1)} collective-permute-done((bf16[48,1024]{1,0:T(8,128)(2,1)S(1)}, bf16[48,1024]{1,0:T(8,128)(2,1)S(1)}, u32[]{:S(2)}, u32[]{:S(2)}) %collective-permute-start.3) | collective-permute-done | bytes 98336 | tf_op jit(solution)/shard_map/ppermute | solution.py:225
  31.7 2.0 %collective-permute-done.5 = bf16[48,1024]{1,0:T(8,128)(2,1)S(1)} collective-permute-done((bf16[48,1024]{1,0:T(8,128)(2,1)S(1)}, bf16[48,1024]{1,0:T(8,128)(2,1)S(1)}, u32[]{:S(2)}, u32[]{:S(2)}) %collective-permute-start.5) | collective-permute-done | bytes 98336 | tf_op jit(solution)/shard_map/ppermute | solution.py:225
  33.7 3.2 %collective-permute-start.6 = (bf16[48,1024]{1,0:T(8,128)(2,1)S(1)}, bf16[48,1024]{1,0:T(8,128)(2,1)S(1)}, u32[]{:S(2)}, u32[]{:S(2)}) collective-permute-start(bf16[48,1024]{1,0:T(8,128)(2,1)S(1)} %fusion.7), channel_id=1, source_target_pairs={{0,4},{1,5},{2,6},{3,7},{4,0},{5,1},{6,2},{7,3},{8,12},{9,13},{10,... | collective-permute-start | bytes 294920 | tf_op jit(solution)/shard_map/ppermute | solution.py:225
  36.9 2.4 %shard_map.114 = (bf16[48,1024]{1,0:T(8,128)(2,1)S(1)}, bf16[48,1024]{1,0:T(8,128)(2,1)S(1)}, bf16[48,1024]{1,0:T(8,128)(2,1)S(1)}, bf16[48,1024]{1,0:T(8,128)(2,1)S(1)}) custom-call(bf16[48,2048]{1,0:T(8,128)(2,1)S(1)} %fusion.1.refs_0_, bf16[2048,512]{1,0:T(8,128)(2,1)S(1)} %bitcast.19, bf16[512,3072]{1,0:T(8,128)(2,1)S(1)} %bitcast.17, ...), custom_call_target="tpu_custom_call" | custom-call | flops 1207959552 | bytes 6291456 | tf_op jit(solution)/shard_map/pallas_call | solution.py:18
  39.4 1.9 %collective-permute-start.9 = (bf16[48,1024]{1,0:T(8,128)(2,1)S(1)}, bf16[48,1024]{1,0:T(8,128)(2,1)S(1)}, u32[]{:S(2)}, u32[]{:S(2)}) collective-permute-start(bf16[48,1024]{1,0:T(8,128)(2,1)S(1)} %get-tuple-element.54), channel_id=1, source_target_pairs={{0,1},{1,0},{2,3},{3,2},{4,5},{5,4},{6,7},{7,6},{8,9},{9,8},{10,11... | collective-permute-start | bytes 294920 | tf_op jit(solution)/shard_map/ppermute | solution.py:225
  41.3 1.6 %collective-permute-start.11 = (bf16[48,1024]{1,0:T(8,128)(2,1)S(1)}, bf16[48,1024]{1,0:T(8,128)(2,1)S(1)}, u32[]{:S(2)}, u32[]{:S(2)}) collective-permute-start(bf16[48,1024]{1,0:T(8,128)(2,1)S(1)} %get-tuple-element.56), channel_id=1, source_target_pairs={{0,3},{1,2},{2,1},{3,0},{4,7},{5,6},{6,5},{7,4},{8,11},{9,10},{10,... | collective-permute-start | bytes 294920 | tf_op jit(solution)/shard_map/ppermute | solution.py:225
  44.4 2.0 %collective-permute-start.14 = (bf16[48,1024]{1,0:T(8,128)(2,1)S(1)}, bf16[48,1024]{1,0:T(8,128)(2,1)S(1)}, u32[]{:S(2)}, u32[]{:S(2)}) collective-permute-start(bf16[48,1024]{1,0:T(8,128)(2,1)S(1)} %multiply_convert_fusion.refs_0_), channel_id=1, source_target_pairs={{0,2},{1,3},{2,0},{3,1},{4,6},{5,7},{6,4},{7,5},{8,10},{9,11},{10,... | collective-permute-start | bytes 294920 | tf_op jit(solution)/shard_map/ppermute | solution.py:225
  46.8 1.8 %collective-permute-done.15.refs_1_ = bf16[48,1024]{1,0:T(8,128)(2,1)S(1)} collective-permute-done((bf16[48,1024]{1,0:T(8,128)(2,1)S(1)}, bf16[48,1024]{1,0:T(8,128)(2,1)S(1)}, u32[]{:S(2)}, u32[]{:S(2)}) %collective-permute-start.15) | collective-permute-done | bytes 98336 | tf_op jit(solution)/shard_map/ppermute | solution.py:225
  51.6 1.6 %collective-permute-start.16 = (bf16[48,512]{1,0:T(8,128)(2,1)S(1)}, bf16[48,512]{1,0:T(8,128)(2,1)S(1)}, u32[]{:S(2)}, u32[]{:S(2)}) collective-permute-start(bf16[48,512]{1,0:T(8,128)(2,1)S(1)} %get-tuple-element.61), channel_id=1, source_target_pairs={{0,8},{1,9},{2,10},{3,11},{4,12},{5,13},{6,14},{7,15},{8,16},{9,17... | collective-permute-start | bytes 147464 | tf_op jit(solution)/shard_map/ppermute | solution.py:379
  53.3 2.4 %collective-permute-start.12 = (bf16[48,1024]{1,0:T(8,128)(2,1)S(1)}, bf16[48,1024]{1,0:T(8,128)(2,1)S(1)}, u32[]{:S(2)}, u32[]{:S(2)}) collective-permute-start(bf16[48,1024]{1,0:T(8,128)(2,1)S(1)} %fusion.6), channel_id=1, source_target_pairs={{0,4},{1,5},{2,6},{3,7},{4,0},{5,1},{6,2},{7,3},{8,12},{9,13},{10,... | collective-permute-start | bytes 294920 | tf_op jit(solution)/shard_map/ppermute | solution.py:225
  55.7 3.6 %collective-permute-done.17 = bf16[48,512]{1,0:T(8,128)(2,1)S(1)} collective-permute-done((bf16[48,512]{1,0:T(8,128)(2,1)S(1)}, bf16[48,512]{1,0:T(8,128)(2,1)S(1)}, u32[]{:S(2)}, u32[]{:S(2)}) %collective-permute-start.17) | collective-permute-done | bytes 49184 | tf_op jit(solution)/shard_map/ppermute | solution.py:380
  60.9 2.6 %collective-permute-start.19 = (bf16[48,1024]{1,0:T(8,128)(2,1)S(1)}, bf16[48,1024]{1,0:T(8,128)(2,1)S(1)}, u32[]{:S(2)}, u32[]{:S(2)}) collective-permute-start(bf16[48,1024]{1,0:T(8,128)(2,1)S(1)} %fusion.4.refs_0_), channel_id=1, source_target_pairs={{0,2},{1,3},{2,0},{3,1},{4,6},{5,7},{6,4},{7,5},{8,10},{9,11},{10,... | collective-permute-start | bytes 294920 | tf_op jit(solution)/shard_map/ppermute | solution.py:225
  64.3 3.1 %collective-permute-done.20.refs_1_ = bf16[48,1024]{1,0:T(8,128)(2,1)S(1)} collective-permute-done((bf16[48,1024]{1,0:T(8,128)(2,1)S(1)}, bf16[48,1024]{1,0:T(8,128)(2,1)S(1)}, u32[]{:S(2)}, u32[]{:S(2)}) %collective-permute-start.20) | collective-permute-done | bytes 98336 | tf_op jit(solution)/shard_map/ppermute | solution.py:225
  (49 shorter events, 14.6 us)
Async XLA Ops:
  0.0 8.1 %collective-permute-start = (bf16[96,1024]{1,0:T(8,128)(2,1)}, bf16[96,1024]{1,0:T(8,128)(2,1)S(1)}, u32[]{:S(2)}, u32[]{:S(2)}) collective-permute-start(bf16[96,1024]{1,0:T(8,128)(2,1)} %bitcast.28), channel_id=1, source_target_pairs={{0,1},{1,0},{2,3},{3,2},{4,5},{5,4},{6,7},{7,6},{8,9},{9,8},{10,11... | collective-permute-start | bytes 589832 | tf_op jit(solution)/shard_map/ppermute | solution.py:225
  9.9 7.3 %collective-permute-start.1 = (bf16[48,2048]{1,0:T(8,128)(2,1)S(1)}, bf16[48,2048]{1,0:T(8,128)(2,1)S(1)}, u32[]{:S(2)}, u32[]{:S(2)}) collective-permute-start(bf16[48,2048]{1,0:T(8,128)(2,1)S(1)} %get-tuple-element.40), channel_id=1, source_target_pairs={{0,1},{1,0},{2,3},{3,2},{4,5},{5,4},{6,7},{7,6},{8,9},{9,8},{10,11... | collective-permute-start | bytes 589832 | tf_op jit(solution)/shard_map/ppermute | solution.py:225
  13.4 10.0 %copy-start.1 = (bf16[1,512,3072]{2,1,0:T(8,128)(2,1)S(1)}, bf16[1,512,3072]{2,1,0:T(8,128)(2,1)}, u32[]{:S(2)}) copy-start(bf16[1,512,3072]{2,1,0:T(8,128)(2,1)} %param.17) | copy-start | bytes 9437188
  13.5 6.8 %collective-permute-start.7 = (bf16[48,2048]{1,0:T(8,128)(2,1)S(1)}, bf16[48,2048]{1,0:T(8,128)(2,1)S(1)}, u32[]{:S(2)}, u32[]{:S(2)}) collective-permute-start(bf16[48,2048]{1,0:T(8,128)(2,1)S(1)} %get-tuple-element.50), channel_id=1, source_target_pairs={{0,2},{1,3},{2,0},{3,1},{4,6},{5,7},{6,4},{7,5},{8,10},{9,11},{10,... | collective-permute-start | bytes 589832 | tf_op jit(solution)/shard_map/ppermute | solution.py:225
  17.2 6.2 %collective-permute-start.2 = (bf16[48,2048]{1,0:T(8,128)(2,1)S(1)}, bf16[48,2048]{1,0:T(8,128)(2,1)S(1)}, u32[]{:S(2)}, u32[]{:S(2)}) collective-permute-start(bf16[48,2048]{1,0:T(8,128)(2,1)S(1)} %add_convert_fusion.3), channel_id=1, source_target_pairs={{0,2},{1,3},{2,0},{3,1},{4,6},{5,7},{6,4},{7,5},{8,10},{9,11},{10,... | collective-permute-start | bytes 589832 | tf_op jit(solution)/shard_map/ppermute | solution.py:225
  20.3 9.1 %collective-permute-start.8 = (bf16[48,2048]{1,0:T(8,128)(2,1)S(1)}, bf16[48,2048]{1,0:T(8,128)(2,1)S(1)}, u32[]{:S(2)}, u32[]{:S(2)}) collective-permute-start(bf16[48,2048]{1,0:T(8,128)(2,1)S(1)} %add_convert_fusion.1), channel_id=1, source_target_pairs={{0,1},{1,0},{2,3},{3,2},{4,5},{5,4},{6,7},{7,6},{8,9},{9,8},{10,11... | collective-permute-start | bytes 589832 | tf_op jit(solution)/shard_map/ppermute | solution.py:225
  25.9 5.7 %collective-permute-start.3 = (bf16[48,1024]{1,0:T(8,128)(2,1)S(1)}, bf16[48,1024]{1,0:T(8,128)(2,1)S(1)}, u32[]{:S(2)}, u32[]{:S(2)}) collective-permute-start(bf16[48,1024]{1,0:T(8,128)(2,1)S(1)} %get-tuple-element.46), channel_id=1, source_target_pairs={{0,1},{1,0},{2,3},{3,2},{4,5},{5,4},{6,7},{7,6},{8,9},{9,8},{10,11... | collective-permute-start | bytes 294920 | tf_op jit(solution)/shard_map/ppermute | solution.py:225
  26.4 5.3 %collective-permute-start.4 = (bf16[48,1024]{1,0:T(8,128)(2,1)S(1)}, bf16[48,1024]{1,0:T(8,128)(2,1)S(1)}, u32[]{:S(2)}, u32[]{:S(2)}) collective-permute-start(bf16[48,1024]{1,0:T(8,128)(2,1)S(1)} %get-tuple-element.47), channel_id=1, source_target_pairs={{0,2},{1,3},{2,0},{3,1},{4,6},{5,7},{6,4},{7,5},{8,10},{9,11},{10,... | collective-permute-start | bytes 294920 | tf_op jit(solution)/shard_map/ppermute | solution.py:225
  28.1 5.5 %collective-permute-start.5 = (bf16[48,1024]{1,0:T(8,128)(2,1)S(1)}, bf16[48,1024]{1,0:T(8,128)(2,1)S(1)}, u32[]{:S(2)}, u32[]{:S(2)}) collective-permute-start(bf16[48,1024]{1,0:T(8,128)(2,1)S(1)} %get-tuple-element.48), channel_id=1, source_target_pairs={{0,3},{1,2},{2,1},{3,0},{4,7},{5,6},{6,5},{7,4},{8,11},{9,10},{10,... | collective-permute-start | bytes 294920 | tf_op jit(solution)/shard_map/ppermute | solution.py:225
  33.7 14.9 %copy-start = (bf16[1,4096,512]{2,1,0:T(8,128)(2,1)S(1)}, bf16[1,4096,512]{2,1,0:T(8,128)(2,1)}, u32[]{:S(2)}) copy-start(bf16[1,4096,512]{2,1,0:T(8,128)(2,1)} %param.18) | copy-start | bytes 12582916
  33.7 9.2 %collective-permute-start.6 = (bf16[48,1024]{1,0:T(8,128)(2,1)S(1)}, bf16[48,1024]{1,0:T(8,128)(2,1)S(1)}, u32[]{:S(2)}, u32[]{:S(2)}) collective-permute-start(bf16[48,1024]{1,0:T(8,128)(2,1)S(1)} %fusion.7), channel_id=1, source_target_pairs={{0,4},{1,5},{2,6},{3,7},{4,0},{5,1},{6,2},{7,3},{8,12},{9,13},{10,... | collective-permute-start | bytes 294920 | tf_op jit(solution)/shard_map/ppermute | solution.py:225
  39.3 11.7 %copy-start.4 = (f32[1,512]{1,0:T(1,128)S(1)}, f32[1,512]{1,0:T(1,128)}, u32[]{:S(2)}) copy-start(f32[1,512]{1,0:T(1,128)} %refs_4_.3) | copy-start | bytes 6148
  39.4 7.1 %collective-permute-start.9 = (bf16[48,1024]{1,0:T(8,128)(2,1)S(1)}, bf16[48,1024]{1,0:T(8,128)(2,1)S(1)}, u32[]{:S(2)}, u32[]{:S(2)}) collective-permute-start(bf16[48,1024]{1,0:T(8,128)(2,1)S(1)} %get-tuple-element.54), channel_id=1, source_target_pairs={{0,1},{1,0},{2,3},{3,2},{4,5},{5,4},{6,7},{7,6},{8,9},{9,8},{10,11... | collective-permute-start | bytes 294920 | tf_op jit(solution)/shard_map/ppermute | solution.py:225
  41.3 5.3 %collective-permute-start.10 = (bf16[48,1024]{1,0:T(8,128)(2,1)S(1)}, bf16[48,1024]{1,0:T(8,128)(2,1)S(1)}, u32[]{:S(2)}, u32[]{:S(2)}) collective-permute-start(bf16[48,1024]{1,0:T(8,128)(2,1)S(1)} %get-tuple-element.55), channel_id=1, source_target_pairs={{0,2},{1,3},{2,0},{3,1},{4,6},{5,7},{6,4},{7,5},{8,10},{9,11},{10,... | collective-permute-start | bytes 294920 | tf_op jit(solution)/shard_map/ppermute | solution.py:225
  41.3 5.5 %collective-permute-start.11 = (bf16[48,1024]{1,0:T(8,128)(2,1)S(1)}, bf16[48,1024]{1,0:T(8,128)(2,1)S(1)}, u32[]{:S(2)}, u32[]{:S(2)}) collective-permute-start(bf16[48,1024]{1,0:T(8,128)(2,1)S(1)} %get-tuple-element.56), channel_id=1, source_target_pairs={{0,3},{1,2},{2,1},{3,0},{4,7},{5,6},{6,5},{7,4},{8,11},{9,10},{10,... | collective-permute-start | bytes 294920 | tf_op jit(solution)/shard_map/ppermute | solution.py:225
  43.0 5.6 %collective-permute-start.15 = (bf16[48,1024]{1,0:T(8,128)(2,1)S(1)}, bf16[48,1024]{1,0:T(8,128)(2,1)S(1)}, u32[]{:S(2)}, u32[]{:S(2)}) collective-permute-start(bf16[48,1024]{1,0:T(8,128)(2,1)S(1)} %multiply_convert_fusion.refs_0_), channel_id=1, source_target_pairs={{0,3},{1,2},{2,1},{3,0},{4,7},{5,6},{6,5},{7,4},{8,11},{9,10},{10,... | collective-permute-start | bytes 294920 | tf_op jit(solution)/shard_map/ppermute | solution.py:225
  44.4 5.7 %collective-permute-start.14 = (bf16[48,1024]{1,0:T(8,128)(2,1)S(1)}, bf16[48,1024]{1,0:T(8,128)(2,1)S(1)}, u32[]{:S(2)}, u32[]{:S(2)}) collective-permute-start(bf16[48,1024]{1,0:T(8,128)(2,1)S(1)} %multiply_convert_fusion.refs_0_), channel_id=1, source_target_pairs={{0,2},{1,3},{2,0},{3,1},{4,6},{5,7},{6,4},{7,5},{8,10},{9,11},{10,... | collective-permute-start | bytes 294920 | tf_op jit(solution)/shard_map/ppermute | solution.py:225
  46.4 4.6 %collective-permute-start.13 = (bf16[48,1024]{1,0:T(8,128)(2,1)S(1)}, bf16[48,1024]{1,0:T(8,128)(2,1)S(1)}, u32[]{:S(2)}, u32[]{:S(2)}) collective-permute-start(bf16[48,1024]{1,0:T(8,128)(2,1)S(1)} %multiply_convert_fusion.refs_0_), channel_id=1, source_target_pairs={{0,1},{1,0},{2,3},{3,2},{4,5},{5,4},{6,7},{7,6},{8,9},{9,8},{10,11... | collective-permute-start | bytes 294920 | tf_op jit(solution)/shard_map/ppermute | solution.py:225
  51.5 7.8 %collective-permute-start.17 = (bf16[48,512]{1,0:T(8,128)(2,1)S(1)}, bf16[48,512]{1,0:T(8,128)(2,1)S(1)}, u32[]{:S(2)}, u32[]{:S(2)}) collective-permute-start(bf16[48,512]{1,0:T(8,128)(2,1)S(1)} %get-tuple-element.61), channel_id=1, source_target_pairs={{0,12},{1,13},{2,14},{3,15},{4,8},{5,9},{6,10},{7,11},{8,20},{9,21... | collective-permute-start | bytes 147464 | tf_op jit(solution)/shard_map/ppermute | solution.py:380
  51.6 7.7 %collective-permute-start.16 = (bf16[48,512]{1,0:T(8,128)(2,1)S(1)}, bf16[48,512]{1,0:T(8,128)(2,1)S(1)}, u32[]{:S(2)}, u32[]{:S(2)}) collective-permute-start(bf16[48,512]{1,0:T(8,128)(2,1)S(1)} %get-tuple-element.61), channel_id=1, source_target_pairs={{0,8},{1,9},{2,10},{3,11},{4,12},{5,13},{6,14},{7,15},{8,16},{9,17... | collective-permute-start | bytes 147464 | tf_op jit(solution)/shard_map/ppermute | solution.py:379
  53.3 7.4 %collective-permute-start.12 = (bf16[48,1024]{1,0:T(8,128)(2,1)S(1)}, bf16[48,1024]{1,0:T(8,128)(2,1)S(1)}, u32[]{:S(2)}, u32[]{:S(2)}) collective-permute-start(bf16[48,1024]{1,0:T(8,128)(2,1)S(1)} %fusion.6), channel_id=1, source_target_pairs={{0,4},{1,5},{2,6},{3,7},{4,0},{5,1},{6,2},{7,3},{8,12},{9,13},{10,... | collective-permute-start | bytes 294920 | tf_op jit(solution)/shard_map/ppermute | solution.py:225
  60.8 6.6 %collective-permute-start.20 = (bf16[48,1024]{1,0:T(8,128)(2,1)S(1)}, bf16[48,1024]{1,0:T(8,128)(2,1)S(1)}, u32[]{:S(2)}, u32[]{:S(2)}) collective-permute-start(bf16[48,1024]{1,0:T(8,128)(2,1)S(1)} %fusion.4.refs_0_), channel_id=1, source_target_pairs={{0,3},{1,2},{2,1},{3,0},{4,7},{5,6},{6,5},{7,4},{8,11},{9,10},{10,... | collective-permute-start | bytes 294920 | tf_op jit(solution)/shard_map/ppermute | solution.py:225
  60.9 7.5 %collective-permute-start.19 = (bf16[48,1024]{1,0:T(8,128)(2,1)S(1)}, bf16[48,1024]{1,0:T(8,128)(2,1)S(1)}, u32[]{:S(2)}, u32[]{:S(2)}) collective-permute-start(bf16[48,1024]{1,0:T(8,128)(2,1)S(1)} %fusion.4.refs_0_), channel_id=1, source_target_pairs={{0,2},{1,3},{2,0},{3,1},{4,6},{5,7},{6,4},{7,5},{8,10},{9,11},{10,... | collective-permute-start | bytes 294920 | tf_op jit(solution)/shard_map/ppermute | solution.py:225
  63.5 5.3 %collective-permute-start.18 = (bf16[48,1024]{1,0:T(8,128)(2,1)S(1)}, bf16[48,1024]{1,0:T(8,128)(2,1)S(1)}, u32[]{:S(2)}, u32[]{:S(2)}) collective-permute-start(bf16[48,1024]{1,0:T(8,128)(2,1)S(1)} %fusion.4.refs_0_), channel_id=1, source_target_pairs={{0,1},{1,0},{2,3},{3,2},{4,5},{5,4},{6,7},{7,6},{8,9},{9,8},{10,11... | collective-permute-start | bytes 294920 | tf_op jit(solution)/shard_map/ppermute | solution.py:225
  (2 other events, 15.1 us)

commit v2 on v1

--- a/solution.py
+++ b/solution.py
@@ -52,17 +52,16 @@
 
 
 def load_kernel(members, group, where, layer, *refs):
-    (inverse, update, rhs, child_maps, parent_maps, root_rhs) = refs[:6]
-    (inverse_v, update_v, partial, child_low, parent_low, columns, parent_columns) = refs[6:13]
-    (placed_rhs, keep, lower_in, upper_in) = refs[13:17]
-    rhs_v, child_maps_v, parent_maps_v, root_rhs_v, sems = refs[17:]
+    (inverse, rhs, child_maps, parent_maps, root_rhs) = refs[:5]
+    (inverse_v, partial, child_low, parent_low, columns, parent_columns) = refs[5:11]
+    (placed_rhs, keep, lower_in, upper_in) = refs[11:15]
+    rhs_v, child_maps_v, parent_maps_v, root_rhs_v, sems = refs[15:]
     pairs = (
         (child_maps, child_maps_v),
         (parent_maps, parent_maps_v),
         (root_rhs, root_rhs_v),
         (rhs, rhs_v),
         (inverse, inverse_v),
-        (update, update_v),
     )
     copies = [pltpu.make_async_copy(a, b, sems.at[i]) for i, (a, b) in enumerate(pairs)]
     for copy in copies:
@@ -93,7 +92,6 @@
     partial[...] = jnp.dot(
         rhs_v[...], inverse_v[pl.ds(own, depth), :], preferred_element_type=F32
     )
-    copies[5].wait()
 
 
 def child_kernel(pieces, base, members, group, where, *refs):
@@ -108,7 +106,7 @@
         depth = piece.shape[1]
         first = pl.multiple_of((place ^ k) * depth, depth)
         solved = solved + jnp.dot(
-            piece[here, :], inverse[pl.ds(first, depth), :], preferred_element_type=F32
+            piece[...], inverse[pl.ds(first, depth), :], preferred_element_type=F32
         )
     solved = solved.astype(BF)
     for start in range(0, update.shape[1], 512):
@@ -229,14 +227,13 @@
     parent_width = parent_update.shape[2]
     root_share = root_size // devices
     hbm = pl.BlockSpec(memory_space=pltpu.HBM)
-    (inverse, update, partial, child_low, parent_low, columns, parent_columns, *masks) = pl.pallas_call(
+    (inverse, partial, child_low, parent_low, columns, parent_columns, *masks) = pl.pallas_call(
         functools.partial(load_kernel, members, group, where, layer),
         name="load",
         out_shape=[
             jax.ShapeDtypeStruct(shape, dtype)
             for shape, dtype in (
                 (child_inverse.shape[1:], BF),
-                (child_update.shape[1:], BF),
                 ((both, child_inverse.shape[2]), F32),
                 ((LOW, child_width), BF),
                 ((LOW, parent_width), BF),
@@ -248,14 +245,14 @@
                 ((1, root_share), F32),
             )
         ],
-        in_specs=[hbm] * 6,
-        out_specs=[WHOLE] * 11,
+        in_specs=[hbm] * 5,
+        out_specs=[WHOLE] * 10,
         scratch_shapes=[
             pltpu.VMEM(rhs.shape, BF),
             pltpu.VMEM(child_map.shape, jnp.int32),
             pltpu.VMEM(parent_map.shape, jnp.int32),
             pltpu.VMEM((both, root_share), BF),
-            pltpu.SemaphoreType.DMA((6,)),
+            pltpu.SemaphoreType.DMA((5,)),
         ],
         compiler_params=pltpu.CompilerParams(vmem_limit_bytes=8 << 20),
         cost_estimate=pl.CostEstimate(
@@ -266,7 +263,6 @@
             pltpu.with_memory_space_constraint(value, pltpu.HBM)
             for value in (
                 child_inverse[0],
-                child_update[0],
                 rhs,
                 child_map,
                 parent_map,
@@ -276,8 +272,6 @@
     )
     placed_rhs, keep, lower_in, upper_in = masks
     own_rhs = parent_rhs[0].reshape(both, parent_rhs.shape[3])
-
-    pieces = [trade(rhs, k) for k in range(1, members)]
 
     def child_part(block):
         return call(
@@ -286,10 +280,10 @@
             [pltpu.VMEM((8 * rows, child_width), BF), pltpu.VMEM((rows, parent_size), F32)],
             8 << 20,
             (rows * 2 * child_inverse.size * 2, child_inverse.size * 4),
-            *pieces,
+            *[trade(rhs[block * rows : (block + 1) * rows], k) for k in range(1, members)],
             partial,
             inverse,
-            update,
+            child_update[0],
             columns,
             child_low,
             own_rhs,
@@ -340,8 +334,8 @@
             total = total + value.astype(F32)
         return total
 
-    early_ones = (0, group - 1)
-    late_ones = tuple(range(1, group - 1))
+    early_ones = (0, *range(2, group))
+    late_ones = (1,)
 
     def gathered(now):
         pieces = [now] + [trade(now, k) for k in range(1, group)]

time: 70.1 us -> 69.7 us (level)
  waiting for transfers between devices: 23.9 us -> 22.2 us
  local copies, waits for them, and re-layouts: 0.03 us -> 1.14 us
  starting transfers between devices: 28.6 us -> 29.7 us
  Pallas kernels: 16.6 us -> 15.8 us
    ppermute x19 -> x20, waiting for transfers between devices: 20.3 us -> 18.1 us  [trade(): return lax.ppermute(value, 'front', [(d, d ^ k) for d in range(devices)])]
    slice x0 -> x1, local copies, waits for them, and re-layouts: none -> 1.1 us  [child_part(): rhs[block * rows:(block + 1) * rows]]
    ppermute x19 -> x20, starting transfers between devices: 26.9 us -> 27.9 us  [trade(): return lax.ppermute(value, 'front', [(d, d ^ k) for d in range(devices)])]
    pallas_call x1, Pallas kernels: 3.74 us -> 2.89 us  [body(): pl.pallas_call(functools.partial(load_kernel, members, group, where, laye...]
  transfers between devices with their start and end apart: 21 -> 22, of which waited for: 14 -> 12; matrix products, arithmetic and copies ran while one was open for 1% -> 1% of each run, Pallas kernels for 19% -> 21%
where the time goes in v2:
time: 69.7 us; the launch traced here: 69.6 us
  starting transfers between devices  29.7 us (43%)
  waiting for transfers between devices  22.2 us (32%)
  Pallas kernels  15.8 us (23%)
  local copies, waits for them, and re-layouts  1.14 us (2%)
    ppermute x20, starting transfers between devices, trade(): return lax.ppermute(value, 'front', [(d, d ^ k) for d in range(devices)])  27.9 us
    ppermute x20, waiting for transfers between devices, trade(): return lax.ppermute(value, 'front', [(d, d ^ k) for d in range(devices)])  18.1 us
    pallas_call x10, Pallas kernels, call(): pl.pallas_call(kernel, out_shape=[jax.ShapeDtypeStruct(shape, dtype) for...  12.9 us
    ppermute x1, waiting for transfers between devices, body(): beside = lax.ppermute(outgoing, ('layer', 'front'), over).astype(F32)  4.05 us
    pallas_call x1, Pallas kernels, body(): pl.pallas_call(functools.partial(load_kernel, members, group, where, laye...  2.89 us
    ppermute x1, starting transfers between devices, body(): incoming = lax.ppermute(outgoing, ('layer', 'front'), same).astype(F32)  1.72 us
  transfers between devices with their start and end apart: 22, of which 12 were waited for; matrix products, arithmetic and copies ran while one was open for 1% of the time, Pallas kernels for 21%

profile of v2, /device:TPU:0, one launch (start us, length us, event | category | flops | bytes accessed | tf_op | source)
XLA Modules:
  0.0 69.6 jit_solution(15459530291392222250)
XLA Ops:
  1.1 3.0 %collective-permute-start = (bf16[48,1024]{1,0:T(8,128)(2,1)S(1)}, bf16[48,1024]{1,0:T(8,128)(2,1)S(1)}, u32[]{:S(2)}, u32[]{:S(2)}) collective-permute-start(bf16[48,1024]{1,0:T(8,128)(2,1)S(1)} %get-tuple-element.64), channel_id=1, source_target_pairs={{0,1},{1,0},{2,3},{3,2},{4,5},{5,4},{6,7},{7,6},{8,9},{9,8},{10,11... | collective-permute-start | bytes 294920 | tf_op jit(solution)/shard_map/ppermute | solution.py:223
  4.2 2.9 %load.1 = (bf16[2048,1024]{1,0:T(8,128)(2,1)S(1)}, f32[96,1024]{1,0:T(8,128)S(1)}, bf16[256,2048]{1,0:T(8,128)(2,1)S(1)}, bf16[256,3072]{1,0:T(8,128)(2,1)S(1)},...) custom-call(bf16[2048,1024]{1,0:T(8,128)(2,1)} %bitcast.32, ...), custom_call_target="tpu_custom_call" | custom-call | flops 201326592 | bytes 16777216 | tf_op jit(solution)/shard_map/load/pallas_call | solution.py:230
  7.6 1.8 %shard_map.109 = (bf16[48,2048]{1,0:T(8,128)(2,1)S(1)}, bf16[48,2048]{1,0:T(8,128)(2,1)S(1)}) custom-call(bf16[48,1024]{1,0:T(8,128)(2,1)S(1)} %collective-permute-done.refs_0_, f32[96,1024]{1,0:T(8,128)S(1)} %get-tuple-element.34.refs_1_, bf16[2048,1024]{1,0:T(8,128)(2,1)S(1)} %get-tuple-element.35.refs_2_, bf16[1024,2048]{1,0:T(8,128)(2,1)S(1)} %bitcast.20, ...), custom_call_target="tpu_custom_call" | custom-call | flops 402653184 | bytes 8388608 | tf_op jit(solution)/shard_map/pallas_call | solution.py:18
  9.4 2.2 %collective-permute-start.1 = (bf16[48,2048]{1,0:T(8,128)(2,1)S(1)}, bf16[48,2048]{1,0:T(8,128)(2,1)S(1)}, u32[]{:S(2)}, u32[]{:S(2)}) collective-permute-start(bf16[48,2048]{1,0:T(8,128)(2,1)S(1)} %get-tuple-element.38), channel_id=1, source_target_pairs={{0,1},{1,0},{2,3},{3,2},{4,5},{5,4},{6,7},{7,6},{8,9},{9,8},{10,11... | collective-permute-start | bytes 589832 | tf_op jit(solution)/shard_map/ppermute | solution.py:223
  11.6 1.8 %shard_map.112 = (bf16[48,2048]{1,0:T(8,128)(2,1)S(1)}, bf16[48,2048]{1,0:T(8,128)(2,1)S(1)}) custom-call(bf16[48,1024]{1,0:T(8,128)(2,1)S(1)} %collective-permute-done.7.refs_0_, f32[96,1024]{1,0:T(8,128)S(1)} %get-tuple-element.34.refs_1_, bf16[2048,1024]{1,0:T(8,128)(2,1)S(1)} %get-tuple-element.35.refs_2_, bf16[1024,2048]{1,0:T(8,128)(2,1)S(1)} %bitcast.21, ...), custom_call_target="tpu_custom_call" | custom-call | flops 402653184 | bytes 8388608 | tf_op jit(solution)/shard_map/pallas_call | solution.py:18
  13.4 1.6 %collective-permute-start.8 = (bf16[48,2048]{1,0:T(8,128)(2,1)S(1)}, bf16[48,2048]{1,0:T(8,128)(2,1)S(1)}, u32[]{:S(2)}, u32[]{:S(2)}) collective-permute-start(bf16[48,2048]{1,0:T(8,128)(2,1)S(1)} %get-tuple-element.48), channel_id=1, source_target_pairs={{0,2},{1,3},{2,0},{3,1},{4,6},{5,7},{6,4},{7,5},{8,10},{9,11},{10,... | collective-permute-start | bytes 589832 | tf_op jit(solution)/shard_map/ppermute | solution.py:223
  17.7 2.7 %collective-permute-done.8 = bf16[48,2048]{1,0:T(8,128)(2,1)S(1)} collective-permute-done((bf16[48,2048]{1,0:T(8,128)(2,1)S(1)}, bf16[48,2048]{1,0:T(8,128)(2,1)S(1)}, u32[]{:S(2)}, u32[]{:S(2)}) %collective-permute-start.8) | collective-permute-done | bytes 196640 | tf_op jit(solution)/shard_map/ppermute | solution.py:223
  20.9 2.4 %collective-permute-done.2 = bf16[48,2048]{1,0:T(8,128)(2,1)S(1)} collective-permute-done((bf16[48,2048]{1,0:T(8,128)(2,1)S(1)}, bf16[48,2048]{1,0:T(8,128)(2,1)S(1)}, u32[]{:S(2)}, u32[]{:S(2)}) %collective-permute-start.2) | collective-permute-done | bytes 196640 | tf_op jit(solution)/shard_map/ppermute | solution.py:223
  23.4 2.4 %shard_map.111 = (bf16[48,1024]{1,0:T(8,128)(2,1)S(1)}, bf16[48,1024]{1,0:T(8,128)(2,1)S(1)}, bf16[48,1024]{1,0:T(8,128)(2,1)S(1)}, bf16[48,1024]{1,0:T(8,128)(2,1)S(1)}) custom-call(bf16[48,2048]{1,0:T(8,128)(2,1)S(1)} %fusion.refs_0_, bf16[2048,512]{1,0:T(8,128)(2,1)S(1)} %bitcast.24, bf16[512,3072]{1,0:T(8,128)(2,1)S(1)} %bitcast.22, ...), custom_call_target="tpu_custom_call" | custom-call | flops 1207959552 | bytes 6291456 | tf_op jit(solution)/shard_map/pallas_call | solution.py:18
  26.0 1.9 %collective-permute-start.4 = (bf16[48,1024]{1,0:T(8,128)(2,1)S(1)}, bf16[48,1024]{1,0:T(8,128)(2,1)S(1)}, u32[]{:S(2)}, u32[]{:S(2)}) collective-permute-start(bf16[48,1024]{1,0:T(8,128)(2,1)S(1)} %get-tuple-element.45), channel_id=1, source_target_pairs={{0,2},{1,3},{2,0},{3,1},{4,6},{5,7},{6,4},{7,5},{8,10},{9,11},{10,... | collective-permute-start | bytes 294920 | tf_op jit(solution)/shard_map/ppermute | solution.py:223
  27.9 1.5 %collective-permute-start.5 = (bf16[48,1024]{1,0:T(8,128)(2,1)S(1)}, bf16[48,1024]{1,0:T(8,128)(2,1)S(1)}, u32[]{:S(2)}, u32[]{:S(2)}) collective-permute-start(bf16[48,1024]{1,0:T(8,128)(2,1)S(1)} %get-tuple-element.46), channel_id=1, source_target_pairs={{0,3},{1,2},{2,1},{3,0},{4,7},{5,6},{6,5},{7,4},{8,11},{9,10},{10,... | collective-permute-start | bytes 294920 | tf_op jit(solution)/shard_map/ppermute | solution.py:223
  29.5 1.8 %collective-permute-done.3 = bf16[48,1024]{1,0:T(8,128)(2,1)S(1)} collective-permute-done((bf16[48,1024]{1,0:T(8,128)(2,1)S(1)}, bf16[48,1024]{1,0:T(8,128)(2,1)S(1)}, u32[]{:S(2)}, u32[]{:S(2)}) %collective-permute-start.3) | collective-permute-done | bytes 98336 | tf_op jit(solution)/shard_map/ppermute | solution.py:223
  31.3 2.2 %collective-permute-done.5 = bf16[48,1024]{1,0:T(8,128)(2,1)S(1)} collective-permute-done((bf16[48,1024]{1,0:T(8,128)(2,1)S(1)}, bf16[48,1024]{1,0:T(8,128)(2,1)S(1)}, u32[]{:S(2)}, u32[]{:S(2)}) %collective-permute-start.5) | collective-permute-done | bytes 98336 | tf_op jit(solution)/shard_map/ppermute | solution.py:223
  33.5 3.3 %collective-permute-start.6 = (bf16[48,1024]{1,0:T(8,128)(2,1)S(1)}, bf16[48,1024]{1,0:T(8,128)(2,1)S(1)}, u32[]{:S(2)}, u32[]{:S(2)}) collective-permute-start(bf16[48,1024]{1,0:T(8,128)(2,1)S(1)} %fusion.7), channel_id=1, source_target_pairs={{0,4},{1,5},{2,6},{3,7},{4,0},{5,1},{6,2},{7,3},{8,12},{9,13},{10,... | collective-permute-start | bytes 294920 | tf_op jit(solution)/shard_map/ppermute | solution.py:223
  36.9 2.4 %shard_map.114 = (bf16[48,1024]{1,0:T(8,128)(2,1)S(1)}, bf16[48,1024]{1,0:T(8,128)(2,1)S(1)}, bf16[48,1024]{1,0:T(8,128)(2,1)S(1)}, bf16[48,1024]{1,0:T(8,128)(2,1)S(1)}) custom-call(bf16[48,2048]{1,0:T(8,128)(2,1)S(1)} %fusion.1.refs_0_, bf16[2048,512]{1,0:T(8,128)(2,1)S(1)} %bitcast.25, bf16[512,3072]{1,0:T(8,128)(2,1)S(1)} %bitcast.23, ...), custom_call_target="tpu_custom_call" | custom-call | flops 1207959552 | bytes 6291456 | tf_op jit(solution)/shard_map/pallas_call | solution.py:18
  40.7 2.1 %collective-permute-start.12 = (bf16[48,1024]{1,0:T(8,128)(2,1)S(1)}, bf16[48,1024]{1,0:T(8,128)(2,1)S(1)}, u32[]{:S(2)}, u32[]{:S(2)}) collective-permute-start(bf16[48,1024]{1,0:T(8,128)(2,1)S(1)} %get-tuple-element.54), channel_id=1, source_target_pairs={{0,3},{1,2},{2,1},{3,0},{4,7},{5,6},{6,5},{7,4},{8,11},{9,10},{10,... | collective-permute-start | bytes 294920 | tf_op jit(solution)/shard_map/ppermute | solution.py:223
  43.8 1.9 %collective-permute-start.15 = (bf16[48,1024]{1,0:T(8,128)(2,1)S(1)}, bf16[48,1024]{1,0:T(8,128)(2,1)S(1)}, u32[]{:S(2)}, u32[]{:S(2)}) collective-permute-start(bf16[48,1024]{1,0:T(8,128)(2,1)S(1)} %multiply_convert_fusion.refs_0_), channel_id=1, source_target_pairs={{0,2},{1,3},{2,0},{3,1},{4,6},{5,7},{6,4},{7,5},{8,10},{9,11},{10,... | collective-permute-start | bytes 294920 | tf_op jit(solution)/shard_map/ppermute | solution.py:223
  46.6 2.0 %collective-permute-done.16.refs_2_ = bf16[48,1024]{1,0:T(8,128)(2,1)S(1)} collective-permute-done((bf16[48,1024]{1,0:T(8,128)(2,1)S(1)}, bf16[48,1024]{1,0:T(8,128)(2,1)S(1)}, u32[]{:S(2)}, u32[]{:S(2)}) %collective-permute-start.16) | collective-permute-done | bytes 98336 | tf_op jit(solution)/shard_map/ppermute | solution.py:223
  50.7 1.7 %collective-permute-start.17 = (bf16[48,512]{1,0:T(8,128)(2,1)S(1)}, bf16[48,512]{1,0:T(8,128)(2,1)S(1)}, u32[]{:S(2)}, u32[]{:S(2)}) collective-permute-start(bf16[48,512]{1,0:T(8,128)(2,1)S(1)} %get-tuple-element.59), channel_id=1, source_target_pairs={{0,8},{1,9},{2,10},{3,11},{4,12},{5,13},{6,14},{7,15},{8,16},{9,17... | collective-permute-start | bytes 147464 | tf_op jit(solution)/shard_map/ppermute | solution.py:373
  52.4 2.4 %collective-permute-start.13 = (bf16[48,1024]{1,0:T(8,128)(2,1)S(1)}, bf16[48,1024]{1,0:T(8,128)(2,1)S(1)}, u32[]{:S(2)}, u32[]{:S(2)}) collective-permute-start(bf16[48,1024]{1,0:T(8,128)(2,1)S(1)} %fusion.6), channel_id=1, source_target_pairs={{0,4},{1,5},{2,6},{3,7},{4,0},{5,1},{6,2},{7,3},{8,12},{9,13},{10,... | collective-permute-start | bytes 294920 | tf_op jit(solution)/shard_map/ppermute | solution.py:223
  54.9 4.1 %collective-permute-done.18 = bf16[48,512]{1,0:T(8,128)(2,1)S(1)} collective-permute-done((bf16[48,512]{1,0:T(8,128)(2,1)S(1)}, bf16[48,512]{1,0:T(8,128)(2,1)S(1)}, u32[]{:S(2)}, u32[]{:S(2)}) %collective-permute-start.18) | collective-permute-done | bytes 49184 | tf_op jit(solution)/shard_map/ppermute | solution.py:374
  59.0 1.6 %collective-permute-done.13 = bf16[48,1024]{1,0:T(8,128)(2,1)S(1)} collective-permute-done((bf16[48,1024]{1,0:T(8,128)(2,1)S(1)}, bf16[48,1024]{1,0:T(8,128)(2,1)S(1)}, u32[]{:S(2)}, u32[]{:S(2)}) %collective-permute-start.13) | collective-permute-done | bytes 98336 | tf_op jit(solution)/shard_map/ppermute | solution.py:223
  60.7 2.4 %collective-permute-start.20 = (bf16[48,1024]{1,0:T(8,128)(2,1)S(1)}, bf16[48,1024]{1,0:T(8,128)(2,1)S(1)}, u32[]{:S(2)}, u32[]{:S(2)}) collective-permute-start(bf16[48,1024]{1,0:T(8,128)(2,1)S(1)} %fusion.4.refs_0_), channel_id=1, source_target_pairs={{0,2},{1,3},{2,0},{3,1},{4,6},{5,7},{6,4},{7,5},{8,10},{9,11},{10,... | collective-permute-start | bytes 294920 | tf_op jit(solution)/shard_map/ppermute | solution.py:223
  64.2 3.1 %collective-permute-done.21.refs_2_ = bf16[48,1024]{1,0:T(8,128)(2,1)S(1)} collective-permute-done((bf16[48,1024]{1,0:T(8,128)(2,1)S(1)}, bf16[48,1024]{1,0:T(8,128)(2,1)S(1)}, u32[]{:S(2)}, u32[]{:S(2)}) %collective-permute-start.21) | collective-permute-done | bytes 98336 | tf_op jit(solution)/shard_map/ppermute | solution.py:223
  (54 shorter events, 14.2 us)
Async XLA Ops:
  1.1 6.5 %collective-permute-start = (bf16[48,1024]{1,0:T(8,128)(2,1)S(1)}, bf16[48,1024]{1,0:T(8,128)(2,1)S(1)}, u32[]{:S(2)}, u32[]{:S(2)}) collective-permute-start(bf16[48,1024]{1,0:T(8,128)(2,1)S(1)} %get-tuple-element.64), channel_id=1, source_target_pairs={{0,1},{1,0},{2,3},{3,2},{4,5},{5,4},{6,7},{7,6},{8,9},{9,8},{10,11... | collective-permute-start | bytes 294920 | tf_op jit(solution)/shard_map/ppermute | solution.py:223
  4.1 7.4 %collective-permute-start.7 = (bf16[48,1024]{1,0:T(8,128)(2,1)S(1)}, bf16[48,1024]{1,0:T(8,128)(2,1)S(1)}, u32[]{:S(2)}, u32[]{:S(2)}) collective-permute-start(bf16[48,1024]{1,0:T(8,128)(2,1)S(1)} %get-tuple-element.63), channel_id=1, source_target_pairs={{0,1},{1,0},{2,3},{3,2},{4,5},{5,4},{6,7},{7,6},{8,9},{9,8},{10,11... | collective-permute-start | bytes 294920 | tf_op jit(solution)/shard_map/ppermute | solution.py:223
  9.4 7.7 %collective-permute-start.1 = (bf16[48,2048]{1,0:T(8,128)(2,1)S(1)}, bf16[48,2048]{1,0:T(8,128)(2,1)S(1)}, u32[]{:S(2)}, u32[]{:S(2)}) collective-permute-start(bf16[48,2048]{1,0:T(8,128)(2,1)S(1)} %get-tuple-element.38), channel_id=1, source_target_pairs={{0,1},{1,0},{2,3},{3,2},{4,5},{5,4},{6,7},{7,6},{8,9},{9,8},{10,11... | collective-permute-start | bytes 589832 | tf_op jit(solution)/shard_map/ppermute | solution.py:223
  13.4 7.0 %collective-permute-start.8 = (bf16[48,2048]{1,0:T(8,128)(2,1)S(1)}, bf16[48,2048]{1,0:T(8,128)(2,1)S(1)}, u32[]{:S(2)}, u32[]{:S(2)}) collective-permute-start(bf16[48,2048]{1,0:T(8,128)(2,1)S(1)} %get-tuple-element.48), channel_id=1, source_target_pairs={{0,2},{1,3},{2,0},{3,1},{4,6},{5,7},{6,4},{7,5},{8,10},{9,11},{10,... | collective-permute-start | bytes 589832 | tf_op jit(solution)/shard_map/ppermute | solution.py:223
  17.1 6.2 %collective-permute-start.2 = (bf16[48,2048]{1,0:T(8,128)(2,1)S(1)}, bf16[48,2048]{1,0:T(8,128)(2,1)S(1)}, u32[]{:S(2)}, u32[]{:S(2)}) collective-permute-start(bf16[48,2048]{1,0:T(8,128)(2,1)S(1)} %add_convert_fusion.3), channel_id=1, source_target_pairs={{0,2},{1,3},{2,0},{3,1},{4,6},{5,7},{6,4},{7,5},{8,10},{9,11},{10,... | collective-permute-start | bytes 589832 | tf_op jit(solution)/shard_map/ppermute | solution.py:223
  20.4 9.0 %collective-permute-start.9 = (bf16[48,2048]{1,0:T(8,128)(2,1)S(1)}, bf16[48,2048]{1,0:T(8,128)(2,1)S(1)}, u32[]{:S(2)}, u32[]{:S(2)}) collective-permute-start(bf16[48,2048]{1,0:T(8,128)(2,1)S(1)} %add_convert_fusion.1), channel_id=1, source_target_pairs={{0,1},{1,0},{2,3},{3,2},{4,5},{5,4},{6,7},{7,6},{8,9},{9,8},{10,11... | collective-permute-start | bytes 589832 | tf_op jit(solution)/shard_map/ppermute | solution.py:223
  25.8 5.4 %collective-permute-start.3 = (bf16[48,1024]{1,0:T(8,128)(2,1)S(1)}, bf16[48,1024]{1,0:T(8,128)(2,1)S(1)}, u32[]{:S(2)}, u32[]{:S(2)}) collective-permute-start(bf16[48,1024]{1,0:T(8,128)(2,1)S(1)} %get-tuple-element.44), channel_id=1, source_target_pairs={{0,1},{1,0},{2,3},{3,2},{4,5},{5,4},{6,7},{7,6},{8,9},{9,8},{10,11... | collective-permute-start | bytes 294920 | tf_op jit(solution)/shard_map/ppermute | solution.py:223
  26.0 5.3 %collective-permute-start.4 = (bf16[48,1024]{1,0:T(8,128)(2,1)S(1)}, bf16[48,1024]{1,0:T(8,128)(2,1)S(1)}, u32[]{:S(2)}, u32[]{:S(2)}) collective-permute-start(bf16[48,1024]{1,0:T(8,128)(2,1)S(1)} %get-tuple-element.45), channel_id=1, source_target_pairs={{0,2},{1,3},{2,0},{3,1},{4,6},{5,7},{6,4},{7,5},{8,10},{9,11},{10,... | collective-permute-start | bytes 294920 | tf_op jit(solution)/shard_map/ppermute | solution.py:223
  27.9 5.5 %collective-permute-start.5 = (bf16[48,1024]{1,0:T(8,128)(2,1)S(1)}, bf16[48,1024]{1,0:T(8,128)(2,1)S(1)}, u32[]{:S(2)}, u32[]{:S(2)}) collective-permute-start(bf16[48,1024]{1,0:T(8,128)(2,1)S(1)} %get-tuple-element.46), channel_id=1, source_target_pairs={{0,3},{1,2},{2,1},{3,0},{4,7},{5,6},{6,5},{7,4},{8,11},{9,10},{10,... | collective-permute-start | bytes 294920 | tf_op jit(solution)/shard_map/ppermute | solution.py:223
  33.5 15.8 %copy-start = (bf16[1,4096,512]{2,1,0:T(8,128)(2,1)S(1)}, bf16[1,4096,512]{2,1,0:T(8,128)(2,1)}, u32[]{:S(2)}) copy-start(bf16[1,4096,512]{2,1,0:T(8,128)(2,1)} %param.18) | copy-start | bytes 12582916
  33.5 9.3 %collective-permute-start.6 = (bf16[48,1024]{1,0:T(8,128)(2,1)S(1)}, bf16[48,1024]{1,0:T(8,128)(2,1)S(1)}, u32[]{:S(2)}, u32[]{:S(2)}) collective-permute-start(bf16[48,1024]{1,0:T(8,128)(2,1)S(1)} %fusion.7), channel_id=1, source_target_pairs={{0,4},{1,5},{2,6},{3,7},{4,0},{5,1},{6,2},{7,3},{8,12},{9,13},{10,... | collective-permute-start | bytes 294920 | tf_op jit(solution)/shard_map/ppermute | solution.py:223
  39.3 11.0 %copy-start.5 = (f32[1,512]{1,0:T(1,128)S(1)}, f32[1,512]{1,0:T(1,128)}, u32[]{:S(2)}) copy-start(f32[1,512]{1,0:T(1,128)} %refs_3_.3) | copy-start | bytes 6148
  39.3 6.4 %collective-permute-start.10 = (bf16[48,1024]{1,0:T(8,128)(2,1)S(1)}, bf16[48,1024]{1,0:T(8,128)(2,1)S(1)}, u32[]{:S(2)}, u32[]{:S(2)}) collective-permute-start(bf16[48,1024]{1,0:T(8,128)(2,1)S(1)} %get-tuple-element.52), channel_id=1, source_target_pairs={{0,1},{1,0},{2,3},{3,2},{4,5},{5,4},{6,7},{7,6},{8,9},{9,8},{10,11... | collective-permute-start | bytes 294920 | tf_op jit(solution)/shard_map/ppermute | solution.py:223
  40.6 6.0 %collective-permute-start.11 = (bf16[48,1024]{1,0:T(8,128)(2,1)S(1)}, bf16[48,1024]{1,0:T(8,128)(2,1)S(1)}, u32[]{:S(2)}, u32[]{:S(2)}) collective-permute-start(bf16[48,1024]{1,0:T(8,128)(2,1)S(1)} %get-tuple-element.53), channel_id=1, source_target_pairs={{0,2},{1,3},{2,0},{3,1},{4,6},{5,7},{6,4},{7,5},{8,10},{9,11},{10,... | collective-permute-start | bytes 294920 | tf_op jit(solution)/shard_map/ppermute | solution.py:223
  40.7 5.8 %collective-permute-start.12 = (bf16[48,1024]{1,0:T(8,128)(2,1)S(1)}, bf16[48,1024]{1,0:T(8,128)(2,1)S(1)}, u32[]{:S(2)}, u32[]{:S(2)}) collective-permute-start(bf16[48,1024]{1,0:T(8,128)(2,1)S(1)} %get-tuple-element.54), channel_id=1, source_target_pairs={{0,3},{1,2},{2,1},{3,0},{4,7},{5,6},{6,5},{7,4},{8,11},{9,10},{10,... | collective-permute-start | bytes 294920 | tf_op jit(solution)/shard_map/ppermute | solution.py:223
  43.0 5.6 %collective-permute-start.16 = (bf16[48,1024]{1,0:T(8,128)(2,1)S(1)}, bf16[48,1024]{1,0:T(8,128)(2,1)S(1)}, u32[]{:S(2)}, u32[]{:S(2)}) collective-permute-start(bf16[48,1024]{1,0:T(8,128)(2,1)S(1)} %multiply_convert_fusion.refs_0_), channel_id=1, source_target_pairs={{0,3},{1,2},{2,1},{3,0},{4,7},{5,6},{6,5},{7,4},{8,11},{9,10},{10,... | collective-permute-start | bytes 294920 | tf_op jit(solution)/shard_map/ppermute | solution.py:223
  43.8 5.5 %collective-permute-start.15 = (bf16[48,1024]{1,0:T(8,128)(2,1)S(1)}, bf16[48,1024]{1,0:T(8,128)(2,1)S(1)}, u32[]{:S(2)}, u32[]{:S(2)}) collective-permute-start(bf16[48,1024]{1,0:T(8,128)(2,1)S(1)} %multiply_convert_fusion.refs_0_), channel_id=1, source_target_pairs={{0,2},{1,3},{2,0},{3,1},{4,6},{5,7},{6,4},{7,5},{8,10},{9,11},{10,... | collective-permute-start | bytes 294920 | tf_op jit(solution)/shard_map/ppermute | solution.py:223
  45.7 4.6 %collective-permute-start.14 = (bf16[48,1024]{1,0:T(8,128)(2,1)S(1)}, bf16[48,1024]{1,0:T(8,128)(2,1)S(1)}, u32[]{:S(2)}, u32[]{:S(2)}) collective-permute-start(bf16[48,1024]{1,0:T(8,128)(2,1)S(1)} %multiply_convert_fusion.refs_0_), channel_id=1, source_target_pairs={{0,1},{1,0},{2,3},{3,2},{4,5},{5,4},{6,7},{7,6},{8,9},{9,8},{10,11... | collective-permute-start | bytes 294920 | tf_op jit(solution)/shard_map/ppermute | solution.py:223
  50.6 8.3 %collective-permute-start.18 = (bf16[48,512]{1,0:T(8,128)(2,1)S(1)}, bf16[48,512]{1,0:T(8,128)(2,1)S(1)}, u32[]{:S(2)}, u32[]{:S(2)}) collective-permute-start(bf16[48,512]{1,0:T(8,128)(2,1)S(1)} %get-tuple-element.59), channel_id=1, source_target_pairs={{0,12},{1,13},{2,14},{3,15},{4,8},{5,9},{6,10},{7,11},{8,20},{9,21... | collective-permute-start | bytes 147464 | tf_op jit(solution)/shard_map/ppermute | solution.py:374
  50.7 8.3 %collective-permute-start.17 = (bf16[48,512]{1,0:T(8,128)(2,1)S(1)}, bf16[48,512]{1,0:T(8,128)(2,1)S(1)}, u32[]{:S(2)}, u32[]{:S(2)}) collective-permute-start(bf16[48,512]{1,0:T(8,128)(2,1)S(1)} %get-tuple-element.59), channel_id=1, source_target_pairs={{0,8},{1,9},{2,10},{3,11},{4,12},{5,13},{6,14},{7,15},{8,16},{9,17... | collective-permute-start | bytes 147464 | tf_op jit(solution)/shard_map/ppermute | solution.py:373
  52.4 8.1 %collective-permute-start.13 = (bf16[48,1024]{1,0:T(8,128)(2,1)S(1)}, bf16[48,1024]{1,0:T(8,128)(2,1)S(1)}, u32[]{:S(2)}, u32[]{:S(2)}) collective-permute-start(bf16[48,1024]{1,0:T(8,128)(2,1)S(1)} %fusion.6), channel_id=1, source_target_pairs={{0,4},{1,5},{2,6},{3,7},{4,0},{5,1},{6,2},{7,3},{8,12},{9,13},{10,... | collective-permute-start | bytes 294920 | tf_op jit(solution)/shard_map/ppermute | solution.py:223
  60.6 6.6 %collective-permute-start.21 = (bf16[48,1024]{1,0:T(8,128)(2,1)S(1)}, bf16[48,1024]{1,0:T(8,128)(2,1)S(1)}, u32[]{:S(2)}, u32[]{:S(2)}) collective-permute-start(bf16[48,1024]{1,0:T(8,128)(2,1)S(1)} %fusion.4.refs_0_), channel_id=1, source_target_pairs={{0,3},{1,2},{2,1},{3,0},{4,7},{5,6},{6,5},{7,4},{8,11},{9,10},{10,... | collective-permute-start | bytes 294920 | tf_op jit(solution)/shard_map/ppermute | solution.py:223
  60.7 7.3 %collective-permute-start.20 = (bf16[48,1024]{1,0:T(8,128)(2,1)S(1)}, bf16[48,1024]{1,0:T(8,128)(2,1)S(1)}, u32[]{:S(2)}, u32[]{:S(2)}) collective-permute-start(bf16[48,1024]{1,0:T(8,128)(2,1)S(1)} %fusion.4.refs_0_), channel_id=1, source_target_pairs={{0,2},{1,3},{2,0},{3,1},{4,6},{5,7},{6,4},{7,5},{8,10},{9,11},{10,... | collective-permute-start | bytes 294920 | tf_op jit(solution)/shard_map/ppermute | solution.py:223
  63.1 5.5 %collective-permute-start.19 = (bf16[48,1024]{1,0:T(8,128)(2,1)S(1)}, bf16[48,1024]{1,0:T(8,128)(2,1)S(1)}, u32[]{:S(2)}, u32[]{:S(2)}) collective-permute-start(bf16[48,1024]{1,0:T(8,128)(2,1)S(1)} %fusion.4.refs_0_), channel_id=1, source_target_pairs={{0,1},{1,0},{2,3},{3,2},{4,5},{5,4},{6,7},{7,6},{8,9},{9,8},{10,11... | collective-permute-start | bytes 294920 | tf_op jit(solution)/shard_map/ppermute | solution.py:223
  (4 other events, 35.2 us)

commit v3 on v2

--- a/solution.py
+++ b/solution.py
@@ -302,7 +302,7 @@
             child_low,
         )
         steps = [1 << bit for bit in range((group - 1).bit_length())]
-        for step in reversed(steps) if block else steps:
+        for step in steps if block else reversed(steps):
             part = (part.astype(F32) + trade(part, step).astype(F32)).astype(BF)
         return call(
             functools.partial(parent_kernel, group, where),
@@ -369,7 +369,10 @@
     )
     places = [(one, d) for one in range(layers) for d in range(devices)]
     same = [(g * devices + d, (g + 1) % layers * devices + d) for g, d in places]
-    over = [(g * devices + d, (g + 1) % layers * devices + (d ^ group)) for g, d in places]
+    over = [
+        (g * devices + d, ((g + 1) % layers if d < group else g) * devices + (d ^ group))
+        for g, d in places
+    ]
     incoming = lax.ppermute(outgoing, ("layer", "front"), same).astype(F32)
     beside = lax.ppermute(outgoing, ("layer", "front"), over).astype(F32)
     arrived = jnp.concatenate([incoming * lower_in + beside * upper_in, incoming * upper_in], 1)

time: 69.7 us -> 69.3 us (level)
  starting transfers between devices: 29.7 us -> 28.2 us
  waiting for transfers between devices: 22.2 us -> 23.1 us
    ppermute x20, waiting for transfers between devices: 18.1 us -> 20.7 us  [trade(): return lax.ppermute(value, 'front', [(d, d ^ k) for d in range(devices)])]
    ppermute x1, waiting for transfers between devices: 4.05 us -> 2.46 us  [body(): beside = lax.ppermute(outgoing, ('layer', 'front'), over).astype(F32)]
    ppermute x20, starting transfers between devices: 27.9 us -> 26.5 us  [trade(): return lax.ppermute(value, 'front', [(d, d ^ k) for d in range(devices)])]
  transfers between devices with their start and end apart: 22 -> 22, of which waited for: 12 -> 14; matrix products, arithmetic and copies ran while one was open for 1% -> 1% of each run, Pallas kernels for 21% -> 21%
where the time goes in v3:
time: 69.3 us; the launch traced here: 69.1 us
  starting transfers between devices  28.2 us (41%)
  waiting for transfers between devices  23.1 us (33%)
  Pallas kernels  15.8 us (23%)
  local copies, waits for them, and re-layouts  1.14 us (2%)
    ppermute x20, starting transfers between devices, trade(): return lax.ppermute(value, 'front', [(d, d ^ k) for d in range(devices)])  26.5 us
    ppermute x20, waiting for transfers between devices, trade(): return lax.ppermute(value, 'front', [(d, d ^ k) for d in range(devices)])  20.7 us
    pallas_call x10, Pallas kernels, call(): pl.pallas_call(kernel, out_shape=[jax.ShapeDtypeStruct(shape, dtype) for...  12.9 us
    pallas_call x1, Pallas kernels, body(): pl.pallas_call(functools.partial(load_kernel, members, group, where, laye...  2.89 us
    ppermute x1, waiting for transfers between devices, body(): beside = lax.ppermute(outgoing, ('layer', 'front'), over).astype(F32)  2.46 us
    ppermute x1, starting transfers between devices, body(): incoming = lax.ppermute(outgoing, ('layer', 'front'), same).astype(F32)  1.65 us
  transfers between devices with their start and end apart: 22, of which 14 were waited for; matrix products, arithmetic and copies ran while one was open for 1% of the time, Pallas kernels for 21%

profile of v3, /device:TPU:0, one launch (start us, length us, event | category | flops | bytes accessed | tf_op | source)
XLA Modules:
  0.0 69.1 jit_solution(203261321740735957)
XLA Ops:
  1.1 3.0 %collective-permute-start = (bf16[48,1024]{1,0:T(8,128)(2,1)S(1)}, bf16[48,1024]{1,0:T(8,128)(2,1)S(1)}, u32[]{:S(2)}, u32[]{:S(2)}) collective-permute-start(bf16[48,1024]{1,0:T(8,128)(2,1)S(1)} %get-tuple-element.64), channel_id=1, source_target_pairs={{0,1},{1,0},{2,3},{3,2},{4,5},{5,4},{6,7},{7,6},{8,9},{9,8},{10,11... | collective-permute-start | bytes 294920 | tf_op jit(solution)/shard_map/ppermute | solution.py:223
  4.2 2.9 %load.1 = (bf16[2048,1024]{1,0:T(8,128)(2,1)S(1)}, f32[96,1024]{1,0:T(8,128)S(1)}, bf16[256,2048]{1,0:T(8,128)(2,1)S(1)}, bf16[256,3072]{1,0:T(8,128)(2,1)S(1)},...) custom-call(bf16[2048,1024]{1,0:T(8,128)(2,1)} %bitcast.32, ...), custom_call_target="tpu_custom_call" | custom-call | flops 201326592 | bytes 16777216 | tf_op jit(solution)/shard_map/load/pallas_call | solution.py:230
  7.6 1.8 %shard_map.109 = (bf16[48,2048]{1,0:T(8,128)(2,1)S(1)}, bf16[48,2048]{1,0:T(8,128)(2,1)S(1)}) custom-call(bf16[48,1024]{1,0:T(8,128)(2,1)S(1)} %collective-permute-done.refs_0_, f32[96,1024]{1,0:T(8,128)S(1)} %get-tuple-element.34.refs_1_, bf16[2048,1024]{1,0:T(8,128)(2,1)S(1)} %get-tuple-element.35.refs_2_, bf16[1024,2048]{1,0:T(8,128)(2,1)S(1)} %bitcast.20, ...), custom_call_target="tpu_custom_call" | custom-call | flops 402653184 | bytes 8388608 | tf_op jit(solution)/shard_map/pallas_call | solution.py:18
  9.4 2.3 %collective-permute-start.1 = (bf16[48,2048]{1,0:T(8,128)(2,1)S(1)}, bf16[48,2048]{1,0:T(8,128)(2,1)S(1)}, u32[]{:S(2)}, u32[]{:S(2)}) collective-permute-start(bf16[48,2048]{1,0:T(8,128)(2,1)S(1)} %get-tuple-element.38), channel_id=1, source_target_pairs={{0,2},{1,3},{2,0},{3,1},{4,6},{5,7},{6,4},{7,5},{8,10},{9,11},{10,... | collective-permute-start | bytes 589832 | tf_op jit(solution)/shard_map/ppermute | solution.py:223
  11.7 1.8 %shard_map.112 = (bf16[48,2048]{1,0:T(8,128)(2,1)S(1)}, bf16[48,2048]{1,0:T(8,128)(2,1)S(1)}) custom-call(bf16[48,1024]{1,0:T(8,128)(2,1)S(1)} %collective-permute-done.7.refs_0_, f32[96,1024]{1,0:T(8,128)S(1)} %get-tuple-element.34.refs_1_, bf16[2048,1024]{1,0:T(8,128)(2,1)S(1)} %get-tuple-element.35.refs_2_, bf16[1024,2048]{1,0:T(8,128)(2,1)S(1)} %bitcast.21, ...), custom_call_target="tpu_custom_call" | custom-call | flops 402653184 | bytes 8388608 | tf_op jit(solution)/shard_map/pallas_call | solution.py:18
  13.5 1.6 %collective-permute-start.8 = (bf16[48,2048]{1,0:T(8,128)(2,1)S(1)}, bf16[48,2048]{1,0:T(8,128)(2,1)S(1)}, u32[]{:S(2)}, u32[]{:S(2)}) collective-permute-start(bf16[48,2048]{1,0:T(8,128)(2,1)S(1)} %get-tuple-element.48), channel_id=1, source_target_pairs={{0,1},{1,0},{2,3},{3,2},{4,5},{5,4},{6,7},{7,6},{8,9},{9,8},{10,11... | collective-permute-start | bytes 589832 | tf_op jit(solution)/shard_map/ppermute | solution.py:223
  17.7 2.8 %collective-permute-done.8 = bf16[48,2048]{1,0:T(8,128)(2,1)S(1)} collective-permute-done((bf16[48,2048]{1,0:T(8,128)(2,1)S(1)}, bf16[48,2048]{1,0:T(8,128)(2,1)S(1)}, u32[]{:S(2)}, u32[]{:S(2)}) %collective-permute-start.8) | collective-permute-done | bytes 196640 | tf_op jit(solution)/shard_map/ppermute | solution.py:223
  20.9 2.5 %collective-permute-done.2 = bf16[48,2048]{1,0:T(8,128)(2,1)S(1)} collective-permute-done((bf16[48,2048]{1,0:T(8,128)(2,1)S(1)}, bf16[48,2048]{1,0:T(8,128)(2,1)S(1)}, u32[]{:S(2)}, u32[]{:S(2)}) %collective-permute-start.2) | collective-permute-done | bytes 196640 | tf_op jit(solution)/shard_map/ppermute | solution.py:223
  23.5 2.4 %shard_map.111 = (bf16[48,1024]{1,0:T(8,128)(2,1)S(1)}, bf16[48,1024]{1,0:T(8,128)(2,1)S(1)}, bf16[48,1024]{1,0:T(8,128)(2,1)S(1)}, bf16[48,1024]{1,0:T(8,128)(2,1)S(1)}) custom-call(bf16[48,2048]{1,0:T(8,128)(2,1)S(1)} %fusion.refs_0_, bf16[2048,512]{1,0:T(8,128)(2,1)S(1)} %bitcast.24, bf16[512,3072]{1,0:T(8,128)(2,1)S(1)} %bitcast.22, ...), custom_call_target="tpu_custom_call" | custom-call | flops 1207959552 | bytes 6291456 | tf_op jit(solution)/shard_map/pallas_call | solution.py:18
  25.9 1.4 %collective-permute-start.3 = (bf16[48,1024]{1,0:T(8,128)(2,1)S(1)}, bf16[48,1024]{1,0:T(8,128)(2,1)S(1)}, u32[]{:S(2)}, u32[]{:S(2)}) collective-permute-start(bf16[48,1024]{1,0:T(8,128)(2,1)S(1)} %get-tuple-element.44), channel_id=1, source_target_pairs={{0,1},{1,0},{2,3},{3,2},{4,5},{5,4},{6,7},{7,6},{8,9},{9,8},{10,11... | collective-permute-start | bytes 294920 | tf_op jit(solution)/shard_map/ppermute | solution.py:223
  27.9 1.5 %collective-permute-start.5 = (bf16[48,1024]{1,0:T(8,128)(2,1)S(1)}, bf16[48,1024]{1,0:T(8,128)(2,1)S(1)}, u32[]{:S(2)}, u32[]{:S(2)}) collective-permute-start(bf16[48,1024]{1,0:T(8,128)(2,1)S(1)} %get-tuple-element.46), channel_id=1, source_target_pairs={{0,3},{1,2},{2,1},{3,0},{4,7},{5,6},{6,5},{7,4},{8,11},{9,10},{10,... | collective-permute-start | bytes 294920 | tf_op jit(solution)/shard_map/ppermute | solution.py:223
  29.6 1.9 %collective-permute-done.3 = bf16[48,1024]{1,0:T(8,128)(2,1)S(1)} collective-permute-done((bf16[48,1024]{1,0:T(8,128)(2,1)S(1)}, bf16[48,1024]{1,0:T(8,128)(2,1)S(1)}, u32[]{:S(2)}, u32[]{:S(2)}) %collective-permute-start.3) | collective-permute-done | bytes 98336 | tf_op jit(solution)/shard_map/ppermute | solution.py:223
  31.9 1.5 %collective-permute-done.5 = bf16[48,1024]{1,0:T(8,128)(2,1)S(1)} collective-permute-done((bf16[48,1024]{1,0:T(8,128)(2,1)S(1)}, bf16[48,1024]{1,0:T(8,128)(2,1)S(1)}, u32[]{:S(2)}, u32[]{:S(2)}) %collective-permute-start.5) | collective-permute-done | bytes 98336 | tf_op jit(solution)/shard_map/ppermute | solution.py:223
  33.5 3.1 %collective-permute-start.6 = (bf16[48,1024]{1,0:T(8,128)(2,1)S(1)}, bf16[48,1024]{1,0:T(8,128)(2,1)S(1)}, u32[]{:S(2)}, u32[]{:S(2)}) collective-permute-start(bf16[48,1024]{1,0:T(8,128)(2,1)S(1)} %fusion.7), channel_id=1, source_target_pairs={{0,4},{1,5},{2,6},{3,7},{4,0},{5,1},{6,2},{7,3},{8,12},{9,13},{10,... | collective-permute-start | bytes 294920 | tf_op jit(solution)/shard_map/ppermute | solution.py:223
  36.7 2.4 %shard_map.114 = (bf16[48,1024]{1,0:T(8,128)(2,1)S(1)}, bf16[48,1024]{1,0:T(8,128)(2,1)S(1)}, bf16[48,1024]{1,0:T(8,128)(2,1)S(1)}, bf16[48,1024]{1,0:T(8,128)(2,1)S(1)}) custom-call(bf16[48,2048]{1,0:T(8,128)(2,1)S(1)} %fusion.1.refs_0_, bf16[2048,512]{1,0:T(8,128)(2,1)S(1)} %bitcast.25, bf16[512,3072]{1,0:T(8,128)(2,1)S(1)} %bitcast.23, ...), custom_call_target="tpu_custom_call" | custom-call | flops 1207959552 | bytes 6291456 | tf_op jit(solution)/shard_map/pallas_call | solution.py:18
  39.1 1.4 %collective-permute-start.10 = (bf16[48,1024]{1,0:T(8,128)(2,1)S(1)}, bf16[48,1024]{1,0:T(8,128)(2,1)S(1)}, u32[]{:S(2)}, u32[]{:S(2)}) collective-permute-start(bf16[48,1024]{1,0:T(8,128)(2,1)S(1)} %get-tuple-element.52), channel_id=1, source_target_pairs={{0,1},{1,0},{2,3},{3,2},{4,5},{5,4},{6,7},{7,6},{8,9},{9,8},{10,11... | collective-permute-start | bytes 294920 | tf_op jit(solution)/shard_map/ppermute | solution.py:223
  40.8 1.8 %collective-permute-start.12 = (bf16[48,1024]{1,0:T(8,128)(2,1)S(1)}, bf16[48,1024]{1,0:T(8,128)(2,1)S(1)}, u32[]{:S(2)}, u32[]{:S(2)}) collective-permute-start(bf16[48,1024]{1,0:T(8,128)(2,1)S(1)} %get-tuple-element.54), channel_id=1, source_target_pairs={{0,3},{1,2},{2,1},{3,0},{4,7},{5,6},{6,5},{7,4},{8,11},{9,10},{10,... | collective-permute-start | bytes 294920 | tf_op jit(solution)/shard_map/ppermute | solution.py:223
  43.9 1.7 %collective-permute-start.15 = (bf16[48,1024]{1,0:T(8,128)(2,1)S(1)}, bf16[48,1024]{1,0:T(8,128)(2,1)S(1)}, u32[]{:S(2)}, u32[]{:S(2)}) collective-permute-start(bf16[48,1024]{1,0:T(8,128)(2,1)S(1)} %multiply_convert_fusion.refs_0_), channel_id=1, source_target_pairs={{0,2},{1,3},{2,0},{3,1},{4,6},{5,7},{6,4},{7,5},{8,10},{9,11},{10,... | collective-permute-start | bytes 294920 | tf_op jit(solution)/shard_map/ppermute | solution.py:223
  46.4 1.9 %collective-permute-done.16.refs_2_ = bf16[48,1024]{1,0:T(8,128)(2,1)S(1)} collective-permute-done((bf16[48,1024]{1,0:T(8,128)(2,1)S(1)}, bf16[48,1024]{1,0:T(8,128)(2,1)S(1)}, u32[]{:S(2)}, u32[]{:S(2)}) %collective-permute-start.16) | collective-permute-done | bytes 98336 | tf_op jit(solution)/shard_map/ppermute | solution.py:223
  50.6 1.7 %collective-permute-start.17 = (bf16[48,512]{1,0:T(8,128)(2,1)S(1)}, bf16[48,512]{1,0:T(8,128)(2,1)S(1)}, u32[]{:S(2)}, u32[]{:S(2)}) collective-permute-start(bf16[48,512]{1,0:T(8,128)(2,1)S(1)} %get-tuple-element.59), channel_id=1, source_target_pairs={{0,8},{1,9},{2,10},{3,11},{4,12},{5,13},{6,14},{7,15},{8,16},{9,17... | collective-permute-start | bytes 147464 | tf_op jit(solution)/shard_map/ppermute | solution.py:376
  53.7 2.5 %collective-permute-done.18 = bf16[48,512]{1,0:T(8,128)(2,1)S(1)} collective-permute-done((bf16[48,512]{1,0:T(8,128)(2,1)S(1)}, bf16[48,512]{1,0:T(8,128)(2,1)S(1)}, u32[]{:S(2)}, u32[]{:S(2)}) %collective-permute-start.18) | collective-permute-done | bytes 49184 | tf_op jit(solution)/shard_map/ppermute | solution.py:377
  56.2 4.2 %collective-permute-done.13 = bf16[48,1024]{1,0:T(8,128)(2,1)S(1)} collective-permute-done((bf16[48,1024]{1,0:T(8,128)(2,1)S(1)}, bf16[48,1024]{1,0:T(8,128)(2,1)S(1)}, u32[]{:S(2)}, u32[]{:S(2)}) %collective-permute-start.13) | collective-permute-done | bytes 98336 | tf_op jit(solution)/shard_map/ppermute | solution.py:223
  60.6 2.3 %collective-permute-start.20 = (bf16[48,1024]{1,0:T(8,128)(2,1)S(1)}, bf16[48,1024]{1,0:T(8,128)(2,1)S(1)}, u32[]{:S(2)}, u32[]{:S(2)}) collective-permute-start(bf16[48,1024]{1,0:T(8,128)(2,1)S(1)} %fusion.4.refs_0_), channel_id=1, source_target_pairs={{0,2},{1,3},{2,0},{3,1},{4,6},{5,7},{6,4},{7,5},{8,10},{9,11},{10,... | collective-permute-start | bytes 294920 | tf_op jit(solution)/shard_map/ppermute | solution.py:223
  64.0 3.1 %collective-permute-done.21.refs_2_ = bf16[48,1024]{1,0:T(8,128)(2,1)S(1)} collective-permute-done((bf16[48,1024]{1,0:T(8,128)(2,1)S(1)}, bf16[48,1024]{1,0:T(8,128)(2,1)S(1)}, u32[]{:S(2)}, u32[]{:S(2)}) %collective-permute-start.21) | collective-permute-done | bytes 98336 | tf_op jit(solution)/shard_map/ppermute | solution.py:223
  (54 shorter events, 15.3 us)
Async XLA Ops:
  1.1 6.5 %collective-permute-start = (bf16[48,1024]{1,0:T(8,128)(2,1)S(1)}, bf16[48,1024]{1,0:T(8,128)(2,1)S(1)}, u32[]{:S(2)}, u32[]{:S(2)}) collective-permute-start(bf16[48,1024]{1,0:T(8,128)(2,1)S(1)} %get-tuple-element.64), channel_id=1, source_target_pairs={{0,1},{1,0},{2,3},{3,2},{4,5},{5,4},{6,7},{7,6},{8,9},{9,8},{10,11... | collective-permute-start | bytes 294920 | tf_op jit(solution)/shard_map/ppermute | solution.py:223
  4.1 7.5 %collective-permute-start.7 = (bf16[48,1024]{1,0:T(8,128)(2,1)S(1)}, bf16[48,1024]{1,0:T(8,128)(2,1)S(1)}, u32[]{:S(2)}, u32[]{:S(2)}) collective-permute-start(bf16[48,1024]{1,0:T(8,128)(2,1)S(1)} %get-tuple-element.63), channel_id=1, source_target_pairs={{0,1},{1,0},{2,3},{3,2},{4,5},{5,4},{6,7},{7,6},{8,9},{9,8},{10,11... | collective-permute-start | bytes 294920 | tf_op jit(solution)/shard_map/ppermute | solution.py:223
  9.4 7.7 %collective-permute-start.1 = (bf16[48,2048]{1,0:T(8,128)(2,1)S(1)}, bf16[48,2048]{1,0:T(8,128)(2,1)S(1)}, u32[]{:S(2)}, u32[]{:S(2)}) collective-permute-start(bf16[48,2048]{1,0:T(8,128)(2,1)S(1)} %get-tuple-element.38), channel_id=1, source_target_pairs={{0,2},{1,3},{2,0},{3,1},{4,6},{5,7},{6,4},{7,5},{8,10},{9,11},{10,... | collective-permute-start | bytes 589832 | tf_op jit(solution)/shard_map/ppermute | solution.py:223
  13.5 7.0 %collective-permute-start.8 = (bf16[48,2048]{1,0:T(8,128)(2,1)S(1)}, bf16[48,2048]{1,0:T(8,128)(2,1)S(1)}, u32[]{:S(2)}, u32[]{:S(2)}) collective-permute-start(bf16[48,2048]{1,0:T(8,128)(2,1)S(1)} %get-tuple-element.48), channel_id=1, source_target_pairs={{0,1},{1,0},{2,3},{3,2},{4,5},{5,4},{6,7},{7,6},{8,9},{9,8},{10,11... | collective-permute-start | bytes 589832 | tf_op jit(solution)/shard_map/ppermute | solution.py:223
  17.1 6.3 %collective-permute-start.2 = (bf16[48,2048]{1,0:T(8,128)(2,1)S(1)}, bf16[48,2048]{1,0:T(8,128)(2,1)S(1)}, u32[]{:S(2)}, u32[]{:S(2)}) collective-permute-start(bf16[48,2048]{1,0:T(8,128)(2,1)S(1)} %add_convert_fusion.3), channel_id=1, source_target_pairs={{0,1},{1,0},{2,3},{3,2},{4,5},{5,4},{6,7},{7,6},{8,9},{9,8},{10,11... | collective-permute-start | bytes 589832 | tf_op jit(solution)/shard_map/ppermute | solution.py:223
  20.6 8.9 %collective-permute-start.9 = (bf16[48,2048]{1,0:T(8,128)(2,1)S(1)}, bf16[48,2048]{1,0:T(8,128)(2,1)S(1)}, u32[]{:S(2)}, u32[]{:S(2)}) collective-permute-start(bf16[48,2048]{1,0:T(8,128)(2,1)S(1)} %add_convert_fusion.1), channel_id=1, source_target_pairs={{0,2},{1,3},{2,0},{3,1},{4,6},{5,7},{6,4},{7,5},{8,10},{9,11},{10,... | collective-permute-start | bytes 589832 | tf_op jit(solution)/shard_map/ppermute | solution.py:223
  25.9 5.5 %collective-permute-start.3 = (bf16[48,1024]{1,0:T(8,128)(2,1)S(1)}, bf16[48,1024]{1,0:T(8,128)(2,1)S(1)}, u32[]{:S(2)}, u32[]{:S(2)}) collective-permute-start(bf16[48,1024]{1,0:T(8,128)(2,1)S(1)} %get-tuple-element.44), channel_id=1, source_target_pairs={{0,1},{1,0},{2,3},{3,2},{4,5},{5,4},{6,7},{7,6},{8,9},{9,8},{10,11... | collective-permute-start | bytes 294920 | tf_op jit(solution)/shard_map/ppermute | solution.py:223
  27.3 4.6 %collective-permute-start.4 = (bf16[48,1024]{1,0:T(8,128)(2,1)S(1)}, bf16[48,1024]{1,0:T(8,128)(2,1)S(1)}, u32[]{:S(2)}, u32[]{:S(2)}) collective-permute-start(bf16[48,1024]{1,0:T(8,128)(2,1)S(1)} %get-tuple-element.45), channel_id=1, source_target_pairs={{0,2},{1,3},{2,0},{3,1},{4,6},{5,7},{6,4},{7,5},{8,10},{9,11},{10,... | collective-permute-start | bytes 294920 | tf_op jit(solution)/shard_map/ppermute | solution.py:223
  27.9 5.5 %collective-permute-start.5 = (bf16[48,1024]{1,0:T(8,128)(2,1)S(1)}, bf16[48,1024]{1,0:T(8,128)(2,1)S(1)}, u32[]{:S(2)}, u32[]{:S(2)}) collective-permute-start(bf16[48,1024]{1,0:T(8,128)(2,1)S(1)} %get-tuple-element.46), channel_id=1, source_target_pairs={{0,3},{1,2},{2,1},{3,0},{4,7},{5,6},{6,5},{7,4},{8,11},{9,10},{10,... | collective-permute-start | bytes 294920 | tf_op jit(solution)/shard_map/ppermute | solution.py:223
  33.5 15.8 %copy-start = (bf16[1,4096,512]{2,1,0:T(8,128)(2,1)S(1)}, bf16[1,4096,512]{2,1,0:T(8,128)(2,1)}, u32[]{:S(2)}) copy-start(bf16[1,4096,512]{2,1,0:T(8,128)(2,1)} %param.18) | copy-start | bytes 12582916
  33.5 9.1 %collective-permute-start.6 = (bf16[48,1024]{1,0:T(8,128)(2,1)S(1)}, bf16[48,1024]{1,0:T(8,128)(2,1)S(1)}, u32[]{:S(2)}, u32[]{:S(2)}) collective-permute-start(bf16[48,1024]{1,0:T(8,128)(2,1)S(1)} %fusion.7), channel_id=1, source_target_pairs={{0,4},{1,5},{2,6},{3,7},{4,0},{5,1},{6,2},{7,3},{8,12},{9,13},{10,... | collective-permute-start | bytes 294920 | tf_op jit(solution)/shard_map/ppermute | solution.py:223
  39.1 11.2 %copy-start.5 = (f32[1,512]{1,0:T(1,128)S(1)}, f32[1,512]{1,0:T(1,128)}, u32[]{:S(2)}) copy-start(f32[1,512]{1,0:T(1,128)} %refs_3_.3) | copy-start | bytes 6148
  39.1 6.5 %collective-permute-start.10 = (bf16[48,1024]{1,0:T(8,128)(2,1)S(1)}, bf16[48,1024]{1,0:T(8,128)(2,1)S(1)}, u32[]{:S(2)}, u32[]{:S(2)}) collective-permute-start(bf16[48,1024]{1,0:T(8,128)(2,1)S(1)} %get-tuple-element.52), channel_id=1, source_target_pairs={{0,1},{1,0},{2,3},{3,2},{4,5},{5,4},{6,7},{7,6},{8,9},{9,8},{10,11... | collective-permute-start | bytes 294920 | tf_op jit(solution)/shard_map/ppermute | solution.py:223
  40.5 5.8 %collective-permute-start.11 = (bf16[48,1024]{1,0:T(8,128)(2,1)S(1)}, bf16[48,1024]{1,0:T(8,128)(2,1)S(1)}, u32[]{:S(2)}, u32[]{:S(2)}) collective-permute-start(bf16[48,1024]{1,0:T(8,128)(2,1)S(1)} %get-tuple-element.53), channel_id=1, source_target_pairs={{0,2},{1,3},{2,0},{3,1},{4,6},{5,7},{6,4},{7,5},{8,10},{9,11},{10,... | collective-permute-start | bytes 294920 | tf_op jit(solution)/shard_map/ppermute | solution.py:223
  40.8 5.6 %collective-permute-start.12 = (bf16[48,1024]{1,0:T(8,128)(2,1)S(1)}, bf16[48,1024]{1,0:T(8,128)(2,1)S(1)}, u32[]{:S(2)}, u32[]{:S(2)}) collective-permute-start(bf16[48,1024]{1,0:T(8,128)(2,1)S(1)} %get-tuple-element.54), channel_id=1, source_target_pairs={{0,3},{1,2},{2,1},{3,0},{4,7},{5,6},{6,5},{7,4},{8,11},{9,10},{10,... | collective-permute-start | bytes 294920 | tf_op jit(solution)/shard_map/ppermute | solution.py:223
  42.7 5.6 %collective-permute-start.16 = (bf16[48,1024]{1,0:T(8,128)(2,1)S(1)}, bf16[48,1024]{1,0:T(8,128)(2,1)S(1)}, u32[]{:S(2)}, u32[]{:S(2)}) collective-permute-start(bf16[48,1024]{1,0:T(8,128)(2,1)S(1)} %multiply_convert_fusion.refs_0_), channel_id=1, source_target_pairs={{0,3},{1,2},{2,1},{3,0},{4,7},{5,6},{6,5},{7,4},{8,11},{9,10},{10,... | collective-permute-start | bytes 294920 | tf_op jit(solution)/shard_map/ppermute | solution.py:223
  43.9 5.4 %collective-permute-start.15 = (bf16[48,1024]{1,0:T(8,128)(2,1)S(1)}, bf16[48,1024]{1,0:T(8,128)(2,1)S(1)}, u32[]{:S(2)}, u32[]{:S(2)}) collective-permute-start(bf16[48,1024]{1,0:T(8,128)(2,1)S(1)} %multiply_convert_fusion.refs_0_), channel_id=1, source_target_pairs={{0,2},{1,3},{2,0},{3,1},{4,6},{5,7},{6,4},{7,5},{8,10},{9,11},{10,... | collective-permute-start | bytes 294920 | tf_op jit(solution)/shard_map/ppermute | solution.py:223
  45.6 4.6 %collective-permute-start.14 = (bf16[48,1024]{1,0:T(8,128)(2,1)S(1)}, bf16[48,1024]{1,0:T(8,128)(2,1)S(1)}, u32[]{:S(2)}, u32[]{:S(2)}) collective-permute-start(bf16[48,1024]{1,0:T(8,128)(2,1)S(1)} %multiply_convert_fusion.refs_0_), channel_id=1, source_target_pairs={{0,1},{1,0},{2,3},{3,2},{4,5},{5,4},{6,7},{7,6},{8,9},{9,8},{10,11... | collective-permute-start | bytes 294920 | tf_op jit(solution)/shard_map/ppermute | solution.py:223
  50.6 5.6 %collective-permute-start.18 = (bf16[48,512]{1,0:T(8,128)(2,1)S(1)}, bf16[48,512]{1,0:T(8,128)(2,1)S(1)}, u32[]{:S(2)}, u32[]{:S(2)}) collective-permute-start(bf16[48,512]{1,0:T(8,128)(2,1)S(1)} %get-tuple-element.59), channel_id=1, source_target_pairs={{0,12},{1,13},{2,14},{3,15},{4,0},{5,1},{6,2},{7,3},{8,20},{9,21},... | collective-permute-start | bytes 147464 | tf_op jit(solution)/shard_map/ppermute | solution.py:377
  50.6 5.5 %collective-permute-start.17 = (bf16[48,512]{1,0:T(8,128)(2,1)S(1)}, bf16[48,512]{1,0:T(8,128)(2,1)S(1)}, u32[]{:S(2)}, u32[]{:S(2)}) collective-permute-start(bf16[48,512]{1,0:T(8,128)(2,1)S(1)} %get-tuple-element.59), channel_id=1, source_target_pairs={{0,8},{1,9},{2,10},{3,11},{4,12},{5,13},{6,14},{7,15},{8,16},{9,17... | collective-permute-start | bytes 147464 | tf_op jit(solution)/shard_map/ppermute | solution.py:376
  52.3 8.1 %collective-permute-start.13 = (bf16[48,1024]{1,0:T(8,128)(2,1)S(1)}, bf16[48,1024]{1,0:T(8,128)(2,1)S(1)}, u32[]{:S(2)}, u32[]{:S(2)}) collective-permute-start(bf16[48,1024]{1,0:T(8,128)(2,1)S(1)} %fusion.6), channel_id=1, source_target_pairs={{0,4},{1,5},{2,6},{3,7},{4,0},{5,1},{6,2},{7,3},{8,12},{9,13},{10,... | collective-permute-start | bytes 294920 | tf_op jit(solution)/shard_map/ppermute | solution.py:223
  60.5 6.6 %collective-permute-start.21 = (bf16[48,1024]{1,0:T(8,128)(2,1)S(1)}, bf16[48,1024]{1,0:T(8,128)(2,1)S(1)}, u32[]{:S(2)}, u32[]{:S(2)}) collective-permute-start(bf16[48,1024]{1,0:T(8,128)(2,1)S(1)} %fusion.4.refs_0_), channel_id=1, source_target_pairs={{0,3},{1,2},{2,1},{3,0},{4,7},{5,6},{6,5},{7,4},{8,11},{9,10},{10,... | collective-permute-start | bytes 294920 | tf_op jit(solution)/shard_map/ppermute | solution.py:223
  60.6 6.7 %collective-permute-start.20 = (bf16[48,1024]{1,0:T(8,128)(2,1)S(1)}, bf16[48,1024]{1,0:T(8,128)(2,1)S(1)}, u32[]{:S(2)}, u32[]{:S(2)}) collective-permute-start(bf16[48,1024]{1,0:T(8,128)(2,1)S(1)} %fusion.4.refs_0_), channel_id=1, source_target_pairs={{0,2},{1,3},{2,0},{3,1},{4,6},{5,7},{6,4},{7,5},{8,10},{9,11},{10,... | collective-permute-start | bytes 294920 | tf_op jit(solution)/shard_map/ppermute | solution.py:223
  62.9 5.3 %collective-permute-start.19 = (bf16[48,1024]{1,0:T(8,128)(2,1)S(1)}, bf16[48,1024]{1,0:T(8,128)(2,1)S(1)}, u32[]{:S(2)}, u32[]{:S(2)}) collective-permute-start(bf16[48,1024]{1,0:T(8,128)(2,1)S(1)} %fusion.4.refs_0_), channel_id=1, source_target_pairs={{0,1},{1,0},{2,3},{3,2},{4,5},{5,4},{6,7},{7,6},{8,9},{9,8},{10,11... | collective-permute-start | bytes 294920 | tf_op jit(solution)/shard_map/ppermute | solution.py:223
  (4 other events, 35.2 us)
